TPU v7x, 32 devices: a whole 2x2x4 slice. The times are simulated.
32 devices in a mesh: dp: 8 (over y, x, core), tp: 4 (over z).
Axes of the slice: x: 2, y: 2, z: 4, core: 2. Of those that a mesh axis runs over, the one named last changes fastest.
Arguments:
- tokens: bfloat16 [8192, 1024], P(('dp', 'tp')), may hold values from -6 to 6
- cotangent: bfloat16 [8192, 1024], P(('dp', 'tp')), may hold values from -6 to 6
- seq_lengths: int32 [8, 2], P('dp'), may hold values from 0 to 1024, as said below
- attention_gain: float32 [1024], replicated, may hold values from 0.5 to 1.5
- query_weight: bfloat16 [1024, 1024], P(None, 'tp'), may hold values from -0.1875 to 0.1875
- latent_down: bfloat16 [1024, 512], replicated, may hold values from -0.1875 to 0.1875
- key_up: bfloat16 [256, 1024], P(None, 'tp'), may hold values from -0.375 to 0.375
- value_up: bfloat16 [256, 1024], P(None, 'tp'), may hold values from -0.375 to 0.375
- out_weight: bfloat16 [1024, 1024], P('tp'), may hold values from -1.5 to 1.5
- feedforward_gain: float32 [1024], replicated, may hold values from 0.5 to 1.5
- gate_weight: bfloat16 [1024, 2816], P(None, 'tp'), may hold values from -0.1875 to 0.1875
- up_weight: bfloat16 [1024, 2816], P(None, 'tp'), may hold values from -0.1875 to 0.1875
- down_weight: bfloat16 [2816, 1024], P('tp'), may hold values from -0.109375 to 0.109375
Outputs:
- output: bfloat16 [8192, 1024], P(('dp', 'tp'))
- tokens_grad: float32 [8192, 1024], P(('dp', 'tp'))
- attention_gain_grad: float32 [1024], P('dp')
- query_weight_grad: float32 [1024, 1024], P('dp', 'tp')
- latent_down_grad: float32 [1024, 512], P('dp', 'tp')
- key_up_grad: float32 [256, 1024], P('dp', 'tp')
- value_up_grad: float32 [256, 1024], P('dp', 'tp')
- out_weight_grad: float32 [1024, 1024], P('tp', 'dp')
- feedforward_gain_grad: float32 [1024], P('dp')
- gate_weight_grad: float32 [1024, 2816], P('dp', 'tp')
- up_weight_grad: float32 [1024, 2816], P('dp', 'tp')
- down_weight_grad: float32 [2816, 1024], P('tp', 'dp')
Inputs may be any that keep to these rules, and one draw needn't show every extreme that they name: `seq_lengths`: row d gives the lengths of the two sequences packed, from row 0 on, into the 1024 tokens of index d of dp; they sum to 1024. Either one sequence fills the pack (second entry 0) or two sequences of half of 1024 each; both kinds occur in every draw.
All inputs are finite; a program needn't handle non-finite values.
Results may differ from a plain program's by a relative error of at most 0.014.
Values may be sent and summed in bfloat16 or wider, within the bound.
No kernel may reach another device: no remote copies, remote signals or barrier semaphores. Data moves between devices by JAX's collectives and lax.ppermute only.
A program may use at most 128 MiB of HBM per device.

v0:
```python
import functools

import jax
import jax.numpy as jnp
from jax import lax
from jax.experimental import pallas as pl
from jax.experimental.pallas import tpu as pltpu
from jax.sharding import PartitionSpec as P


HD = 64
norm_eps = 1e-06
masked_score = -1000000000.0
bf16 = jnp.bfloat16
f32 = jnp.float32


def matmul(left, right):
    return jnp.dot(left, right, preferred_element_type=f32)


def contract_rows(left, right):
    return lax.dot_general(left, right, (((0,), (0,)), ((), ())), preferred_element_type=f32)


def contract_cols(left, right):
    return lax.dot_general(left, right, (((1,), (1,)), ((), ())), preferred_element_type=f32)


def normalize(values):
    factor = lax.rsqrt(jnp.mean(values * values, axis=-1, keepdims=True) + norm_eps)
    return (values * factor, factor)


def norm_backward(upstream, normed, factor, scaling):
    weighted = scaling * upstream
    inner = jnp.mean(weighted * normed, axis=-1, keepdims=True)
    return (factor * (weighted - normed * inner), jnp.sum(upstream * normed, axis=0))


def swap(block, axis, bit):
    count = lax.axis_size(axis)
    return lax.ppermute(block, axis, [(i, i ^ (1 << bit)) for i in range(count)])


def ring(block, step):
    count = lax.axis_size("tp")
    return lax.ppermute(block, "tp", [(i, (i + step) % count) for i in range(count)])


def pick(block, index, axis):
    return lax.dynamic_index_in_dim(block, index, axis, keepdims=False)


def rounded_sum(left, right):
    return (left.astype(f32) + right.astype(f32)).astype(bf16)


def gather_bits(block, bits, dp):
    for bit in bits:
        mine = (dp >> bit) & 1
        other = swap(block, "dp", bit)
        first = jnp.where(mine == 0, block, other)
        second = jnp.where(mine == 0, other, block)
        block = jnp.stack([first, second])
    return block


def halve(block, bit, axis, dp):
    mine = (dp >> bit) & 1
    keep = pick(block, mine, axis)
    send = pick(block, 1 - mine, axis)
    return rounded_sum(keep, swap(send, "dp", bit))


def forward_kernel(info, q_ref, k_ref, v_ref, o_ref, w_ref, bias_ref):
    rows, keys = bias_ref.shape

    @pl.when(pl.program_id(0) == 0)
    def _():
        edge = info[0]
        for k in range(keys // rows):
            row = lax.broadcasted_iota(jnp.int32, (rows, rows), 0) + info[1]
            col = lax.broadcasted_iota(jnp.int32, (rows, rows), 1) + info[1 + k]
            same = (col >= edge).astype(jnp.int32) == (row >= edge).astype(jnp.int32)
            bias_ref[:, k * rows : (k + 1) * rows] = jnp.where(same & (col <= row), 0.0, masked_score)

    outs = []
    for j in range(2):
        lanes = slice(j * HD, (j + 1) * HD)
        scores = contract_cols(q_ref[:, lanes], k_ref[:, lanes]) * (HD**-0.5) + bias_ref[...]
        top = jnp.max(scores, axis=-1, keepdims=True)
        shifted = jnp.exp(scores - top)
        total = jnp.sum(shifted, axis=-1, keepdims=True)
        weights = (shifted * (1.0 / total)).astype(bf16)
        w_ref[j] = weights
        outs.append(matmul(weights, v_ref[:, lanes]).astype(bf16))
    o_ref[...] = jnp.concatenate(outs, axis=1)


def backward_kernel(q_ref, k_ref, v_ref, g_ref, w_ref, dq_ref, dk_ref, dv_ref):
    dqs, dks, dvs = [], [], []
    for j in range(2):
        lanes = slice(j * HD, (j + 1) * HD)
        weights = w_ref[j]
        probs = weights.astype(f32)
        grad = g_ref[:, lanes]
        grad_weights = contract_cols(grad, v_ref[:, lanes])
        delta = jnp.sum(probs * grad_weights, axis=-1, keepdims=True)
        grad_scores = (probs * (grad_weights - delta)).astype(bf16)
        dqs.append((matmul(grad_scores, k_ref[:, lanes]) * (HD**-0.5)).astype(bf16))
        dks.append((contract_rows(grad_scores, q_ref[:, lanes]) * (HD**-0.5)).astype(bf16))
        dvs.append(contract_rows(weights, grad).astype(bf16))
    dq_ref[...] = jnp.concatenate(dqs, axis=1)
    dk_ref[...] = jnp.concatenate(dks, axis=1)
    dv_ref[...] = jnp.concatenate(dvs, axis=1)


def attend_forward(queries, keys, values, info, half):
    rows, width = queries.shape
    total = keys.shape[0]
    pairs = width // (4 * HD)
    width = width // 2
    skip = half * pairs
    small = pl.BlockSpec((rows, 2 * HD), lambda h, s: (0, h))
    part = pl.BlockSpec((rows, 2 * HD), lambda h, s: (0, skip + h))
    large = pl.BlockSpec((total, 2 * HD), lambda h, s: (0, skip + h))
    return pl.pallas_call(
        forward_kernel,
        grid_spec=pltpu.PrefetchScalarGridSpec(
            num_scalar_prefetch=1,
            grid=(pairs,),
            in_specs=[part, large, large],
            out_specs=[small, pl.BlockSpec((2, rows, total), lambda h, s: (h, 0, 0))],
            scratch_shapes=[pltpu.VMEM((rows, total), f32)],
        ),
        out_shape=[
            jax.ShapeDtypeStruct((rows, width), bf16),
            jax.ShapeDtypeStruct((2 * pairs, rows, total), bf16),
        ],
        name="attend_forward",
    )(info, queries, keys, values)


def attend_backward(queries, keys, values, grad, weights, half):
    rows, width = queries.shape
    total = keys.shape[0]
    pairs = width // (4 * HD)
    width = width // 2
    skip = half * pairs
    small = pl.BlockSpec((rows, 2 * HD), lambda h: (0, h))
    large = pl.BlockSpec((total, 2 * HD), lambda h: (0, h))
    part = pl.BlockSpec((rows, 2 * HD), lambda h: (0, skip + h))
    deep = pl.BlockSpec((total, 2 * HD), lambda h: (0, skip + h))
    return pl.pallas_call(
        backward_kernel,
        grid=(pairs,),
        in_specs=[part, deep, deep, part, pl.BlockSpec((2, rows, total), lambda h: (h, 0, 0))],
        out_specs=[small, large, large],
        out_shape=[
            jax.ShapeDtypeStruct((rows, width), bf16),
            jax.ShapeDtypeStruct((total, width), bf16),
            jax.ShapeDtypeStruct((total, width), bf16),
        ],
        name="attend_backward",
    )(queries, keys, values, grad, weights)


def feed_kernel(with_start, with_send, *refs):
    x_ref, g_ref, w_ref = refs[:3]
    starts = refs[3:5] if with_start else ()
    dh_ref, act_ref, out_ref, dx_ref = refs[3 + len(starts) : 7 + len(starts)]
    pad = act_ref.shape[2]
    weights = w_ref[0]
    gate_up = weights[:, : 2 * pad]
    down_t = weights[:, 2 * pad :]
    hidden = matmul(x_ref[...], gate_up)
    gate, up = hidden[:, :pad], hidden[:, pad:]
    sigmoid = jax.nn.sigmoid(gate)
    silu = gate * sigmoid
    act = (silu * up).astype(bf16)
    act_ref[0] = act
    grad_act = matmul(g_ref[...], down_t)
    grad_gate = (grad_act * up * sigmoid * (1.0 + gate * (1.0 - sigmoid))).astype(bf16)
    grad_up = (grad_act * silu).astype(bf16)
    grad_hidden = jnp.concatenate([grad_gate, grad_up], axis=1)
    dh_ref[0] = grad_hidden

    @pl.when(pl.program_id(0) == 0)
    def _():
        if with_start:
            out_ref[...] = starts[0][...]
            dx_ref[...] = starts[1][...]
        else:
            out_ref[...] = jnp.zeros_like(out_ref)
            dx_ref[...] = jnp.zeros_like(dx_ref)

    out_ref[...] += contract_cols(act, down_t)
    dx_ref[...] += contract_cols(grad_hidden, gate_up)
    if not with_start:

        @pl.when(pl.program_id(0) == 0)
        def _():
            refs[-2][...] = x_ref[...].T
            refs[-1][...] = g_ref[...].T

    if with_send:

        @pl.when(pl.program_id(0) == pl.num_programs(0) - 1)
        def _():
            half = out_ref.shape[0] // 2
            refs[-2][...] = out_ref[half:, :].astype(bf16)
            refs[-1][...] = dx_ref[half:, :].astype(bf16)


def feed_forward(both_two, both_up, weights, starts=(), with_send=False):
    count, model, lanes = weights.shape
    rows = both_two.shape[0]
    pad = lanes // 3
    whole = pl.BlockSpec((rows, model), lambda k: (0, 0))
    extra = (rows // 2, model) if with_send else (model, rows)
    return pl.pallas_call(
        functools.partial(feed_kernel, len(starts) > 0, with_send),
        grid=(count,),
        in_specs=[whole, whole, pl.BlockSpec((1, model, lanes), lambda k: (k, 0, 0))] + [whole] * len(starts),
        out_specs=[
            pl.BlockSpec((1, rows, 2 * pad), lambda k: (k, 0, 0)),
            pl.BlockSpec((1, rows, pad), lambda k: (k, 0, 0)),
            whole,
            whole,
        ]
        + [pl.BlockSpec(extra, lambda k: (0, 0))] * 2,
        out_shape=[
            jax.ShapeDtypeStruct((count, rows, 2 * pad), bf16),
            jax.ShapeDtypeStruct((count, rows, pad), bf16),
            jax.ShapeDtypeStruct((rows, model), f32),
            jax.ShapeDtypeStruct((rows, model), f32),
        ]
        + [jax.ShapeDtypeStruct(extra, bf16)] * 2,
        name="feed_forward",
    )(both_two, both_up, weights, *starts)


def feed_grad_kernel(spots, *refs):
    dh_ref, act_ref, a_ref, b_ref = refs[8:]
    pad = act_ref.shape[2]
    half = a_ref.shape[1]
    left = jnp.concatenate([ref[...] for ref in refs[:4]], axis=0)
    both = matmul(left, dh_ref[0]).astype(bf16)
    a_ref[0, :, : 2 * pad] = both[:half]
    b_ref[0, :, : 2 * pad] = both[half:]
    left = jnp.concatenate([ref[...] for ref in refs[4:8]], axis=0)
    both = matmul(left, act_ref[0]).astype(bf16)
    a_ref[0, :, 2 * pad :] = both[:half]
    b_ref[0, :, 2 * pad :] = both[half:]


def feed_grads(spots, two_turned, up_turned, grad_hidden, act):
    model, rows = two_turned.shape
    count, _, pad = act.shape
    block = model // 8
    spot_specs = [pl.BlockSpec((block, rows), functools.partial(lambda i, k, s: (s[i], 0), i)) for i in range(4)]
    out = pl.BlockSpec((1, 2 * block, 3 * pad), lambda k, s: (k, 0, 0))
    return pl.pallas_call(
        feed_grad_kernel,
        grid_spec=pltpu.PrefetchScalarGridSpec(
            num_scalar_prefetch=1,
            grid=(count,),
            in_specs=spot_specs
            + spot_specs
            + [
                pl.BlockSpec((1, rows, 2 * pad), lambda k, s: (k, 0, 0)),
                pl.BlockSpec((1, rows, pad), lambda k, s: (k, 0, 0)),
            ],
            out_specs=[out, out],
        ),
        out_shape=[jax.ShapeDtypeStruct((count, 2 * block, 3 * pad), bf16)] * 2,
        name="feed_grads",
    )(spots, *([two_turned] * 4), *([up_turned] * 4), grad_hidden, act)


def tie(*arrays):
    return lax.optimization_barrier(arrays)


def local(
    tokens,
    cotangent,
    seq_lengths,
    attention_gain,
    query_weight,
    latent_down,
    key_up,
    value_up,
    out_weight,
    feedforward_gain,
    gate_weight,
    up_weight,
    down_weight,
):
    tp = lax.axis_index("tp")
    dp = lax.axis_index("dp")
    planes = lax.axis_size("tp")
    dp_count = lax.axis_size("dp")
    dp_bits = dp_count.bit_length() - 1
    core, xbit, ybit = (dp & 1, (dp >> 1) & 1, (dp >> 2) & 1)
    eighth = dp & 7
    rows, model = tokens.shape
    lat_width, quarter = key_up.shape
    width = planes * quarter
    high = dp_count // 8
    part = model // dp_count
    block = model // 8
    up_part = lat_width // dp_count
    plane_of = [(tp + planes - k) % planes for k in range(planes)]
    boundary = seq_lengths[0, 0]

    def ring_gather(piece):
        got = [piece]
        for _ in range(1, planes):
            got.append(ring(got[-1], 1))
        return got

    def blocks_first(array):
        if high == 1:
            return array
        shaped = array.reshape(array.shape[0], high, 8, part)
        return shaped.transpose(0, 2, 1, 3).reshape(array.shape)

    q_piece = lax.dynamic_slice_in_dim(query_weight, eighth * block, block, 0)

    inputs = tokens.astype(f32)
    normed_one, factor_one = normalize(inputs)
    rows_one = (normed_one * attention_gain).astype(bf16)
    latent_own = matmul(rows_one, latent_down).astype(bf16)
    up_piece = jnp.where(core == 0, key_up, value_up)
    o_piece = lax.dynamic_slice_in_dim(out_weight, eighth * block, block, 1)
    lat_up = jnp.concatenate([latent_own, up_piece, o_piece], axis=1)
    q_list, lat_got = [q_piece], [lat_up]
    q_list.append(ring(q_piece, 1))
    lat_got.append(ring(lat_up, 1))
    q_list.append(ring(q_list[1], 1))
    q_next, lat_next = tie(q_list[2], lat_got[1])
    q_list.append(ring(q_next, 1))
    lat_got.append(ring(lat_next, 1))
    q_all = gather_bits(jnp.stack(q_list), (1,), dp)
    q_all, lat_next = tie(q_all, lat_got[2])
    q_all = gather_bits(q_all, (2, 0), dp)
    lat_got.append(ring(lat_next, 1))
    latents = jnp.concatenate([got[:, : 2 * lat_width] for got in lat_got], axis=0)
    up_mine = jnp.concatenate([got[:, 2 * lat_width : 2 * lat_width + quarter] for got in lat_got], axis=1)
    up_other = swap(up_mine, "dp", 0)
    keys_up = jnp.where(core == 0, up_mine, up_other)
    values_up = jnp.where(core == 0, up_other, up_mine)
    groups = [plane_of[k] * 2 // planes for k in range(planes)]
    group_row = jnp.concatenate(
        [jnp.full((1, quarter), 1, jnp.int32) * groups[k].astype(jnp.int32) for k in range(planes)], axis=1
    )

    def both_groups(array):
        zero = jnp.zeros_like(array)
        return jnp.concatenate([jnp.where(group_row == g, array, zero) for g in range(2)], axis=0)

    keys_wide, values_wide = both_groups(keys_up), both_groups(values_up)

    query_full = q_all.transpose(1, 2, 0, 4, 3, 5).reshape(model, width)

    gate_weight, _ = tie(gate_weight, q_list[1])
    up_weight, _ = tie(up_weight, q_list[3])
    down_weight, _ = tie(down_weight, lat_got[2])
    ff_half = gate_weight.shape[1] // 2
    ff_pad = -(-ff_half // 128) * 128

    def core_half(array):
        chosen = jnp.where(core == 0, array[:, :ff_half], array[:, ff_half:])
        return jnp.pad(chosen, ((0, 0), (0, ff_pad - ff_half)))

    down_half = lax.dynamic_slice_in_dim(down_weight, core * ff_half, ff_half, 0)
    down_turned = jnp.pad(down_half.T, ((0, 0), (0, ff_pad - ff_half)))
    ff_own = jnp.concatenate([core_half(gate_weight), core_half(up_weight), down_turned], axis=1)
    spot = (dp >> 1) & 3
    turned_spot = xbit * 2 + ybit
    ff_a = lax.dynamic_slice_in_dim(ff_own, spot * block, block, 0)
    ff_b = lax.dynamic_slice_in_dim(ff_own, model // 2 + turned_spot * block, block, 0)
    ff_piece, _ = tie(jnp.concatenate([ff_a, ff_b], axis=0), lat_got[planes - 1])
    ff_pieces = ring_gather(ff_piece)
    ff_weights = [ff_own]
    for k in range(1, planes):
        top = gather_bits(ff_pieces[k][:block], (1, 2), dp).reshape(model // 2, 3 * ff_pad)
        bottom = gather_bits(ff_pieces[k][block:], (2, 1), dp).reshape(model // 2, 3 * ff_pad)
        ff_weights.append(jnp.concatenate([top, bottom], axis=0))
    cut = planes // 2
    ff_early, ff_late = jnp.stack(ff_weights[:cut]), jnp.stack(ff_weights[cut:])

    o_got = jnp.concatenate([got[:, 2 * lat_width + quarter :] for got in lat_got], axis=0)
    o_got = gather_bits(o_got, (1, 2, 0), dp)
    out_full = o_got.transpose(3, 1, 2, 0, 4).reshape(width, model)

    queries = matmul(rows_one, query_full).astype(bf16)
    keys = matmul(latents, keys_wide).astype(bf16)
    values = matmul(latents, values_wide).astype(bf16)
    queries, out_full = tie(queries, out_full)
    info = jnp.stack([boundary] + [plane_of[k].astype(jnp.int32) * rows for k in range(planes)])
    attended, weights = [], []
    for half in range(2):
        got, kept_weights = attend_forward(queries, keys, values, info, half)
        attended.append(got)
        weights.append(kept_weights)
    attended = jnp.concatenate(attended, axis=1)
    mixed = inputs + matmul(attended, out_full)
    normed_two, factor_two = normalize(mixed)
    rows_two = (normed_two * feedforward_gain).astype(bf16)

    both_two = jnp.concatenate([rows_two, swap(rows_two, "dp", 0)], axis=0)
    both_up = jnp.concatenate([cotangent, swap(cotangent, "dp", 0)], axis=0)

    def rows_first(array):
        if high == 1:
            return array
        shaped = array.reshape(high, 8, part, array.shape[1])
        return shaped.transpose(1, 0, 2, 3).reshape(array.shape)

    def ff_blocks(which, grads):
        spots = jnp.stack([eighth ^ b for b in which]).astype(jnp.int32)
        return feed_grads(spots, *lefts, *grads)

    sent = (2, 6, 5, 7)
    kept = (0, 4, 1, 3)

    def high_bits(array):
        for bit in range(dp_bits - 1, 2, -1):
            array = array.reshape((2, -1) + array.shape[1:])
            array = halve(array, bit, 0, dp)
        return array.reshape(array.shape[1:])

    def finish(side_a, side_b):
        if high > 1:
            count = side_a.shape[0]
            both = jnp.stack([side_a, side_b], axis=2).reshape(count, high, part, 2, 3 * ff_pad)
            both = high_bits(both.transpose(1, 2, 0, 3, 4))
            side_a, side_b = both[:, :, 0].transpose(1, 0, 2), both[:, :, 1].transpose(1, 0, 2)
        return [jnp.stack([side_a[k], side_b[k]]) for k in range(side_a.shape[0])]

    *early_grads, out_sum, grad_sum, two_turned, up_turned = feed_forward(both_two, both_up, ff_early)
    lefts = (rows_first(two_turned), rows_first(up_turned))
    send_a, send_b = ff_blocks(sent, early_grads)
    send_a, send_b, ff_late = tie(send_a, send_b, ff_late)
    early_a, early_b = swap(send_a, "dp", 1), swap(send_b, "dp", 2)
    *late_grads, out_sum, grad_sum, out_send, grad_send = feed_forward(
        both_two, both_up, ff_late, (out_sum, grad_sum), True
    )
    grad_two = grad_sum[:rows] + swap(grad_send, "dp", 0).astype(f32)
    send_a, send_b = ff_blocks(sent, late_grads)
    late_a, late_b = swap(send_a, "dp", 1), swap(send_b, "dp", 2)
    back_two, gain_two = norm_backward(grad_two, normed_two, factor_two, feedforward_gain)
    grad_mixed = cotangent.astype(f32) + back_two
    output = (mixed + out_sum[:rows] + swap(out_send, "dp", 0).astype(f32)).astype(bf16)

    near = (0, 4, 2, 6)
    far = (1, 5, 3, 7)

    def columns(array, blocks):
        array = blocks_first(array)
        return jnp.concatenate(
            [lax.dynamic_slice_in_dim(array, (eighth ^ b) * block, block, 1) for b in blocks], axis=1
        )

    def block_rows(array, blocks):
        shaped = array.reshape(high, 8, up_part, array.shape[1])
        return jnp.stack(
            [pick(shaped, eighth ^ b, 1).reshape(high * up_part, array.shape[1]) for b in blocks]
        )

    def plane_sum(take):
        parts = [take(r) for r in range(planes)]
        bit = planes.bit_length() - 2
        while len(parts) > 1:
            half = len(parts) // 2
            got = swap(jnp.concatenate([p.astype(bf16) for p in parts[half:]], axis=1), "tp", bit)
            size = parts[0].shape[1]
            parts = [parts[i].astype(f32) + got[:, i * size : (i + 1) * size].astype(f32) for i in range(half)]
            bit -= 1
        return parts[0]

    def ring_columns(array):
        return lambda r: lax.dynamic_slice_in_dim(
            array, ((tp - (tp ^ r) + planes) % planes) * quarter, quarter, 1
        )

    mixed_rows = grad_mixed.astype(bf16)
    grad_attended = contract_cols(mixed_rows, out_full).astype(bf16)
    out_part = contract_rows(mixed_rows, attended).astype(bf16)
    out_part = lax.psum_scatter(out_part, "dp", scatter_dimension=0, tiled=True)

    grad_attended, _, _ = tie(grad_attended, send_a, send_b)

    def back(half, grad):
        return attend_backward(queries, keys, values, grad, weights[half], half)

    def kept_blocks(grads):
        return ff_blocks(kept, grads)

    first_back = back(0, grad_attended)
    early_hidden, early_act, first_query = tie(*early_grads, first_back[0])
    keep_a, keep_b = kept_blocks((early_hidden, early_act))
    next_a = rounded_sum(keep_a[:, block:], early_a[:, block:])
    next_b = rounded_sum(keep_b[:, block:], early_b[:, block:])
    grad_attended, next_a, next_b = tie(grad_attended, next_a, next_b)
    early_next_a, early_next_b = swap(next_a, "dp", 2), swap(next_b, "dp", 1)
    own_a = rounded_sum(keep_a[:, :block], early_a[:, :block])
    own_b = rounded_sum(keep_b[:, :block], early_b[:, :block])
    second_back = back(1, grad_attended)
    grad_queries, grad_keys, grad_values = [
        jnp.concatenate(pair, axis=1) for pair in zip((first_query, *first_back[1:]), second_back)
    ]
    latent_part = (contract_cols(grad_keys, keys_wide) + contract_cols(grad_values, values_wide)).astype(bf16)
    late_hidden, late_act, latent_part = tie(*late_grads, latent_part)

    def lat_rows(k):
        return latent_part[k * rows : (k + 1) * rows]

    lat_one = ring(lat_rows(3), -1)
    keep_a, keep_b = kept_blocks((late_hidden, late_act))
    next_a = rounded_sum(keep_a[:, block:], late_a[:, block:])
    next_b = rounded_sum(keep_b[:, block:], late_b[:, block:])
    late_queries, next_a, next_b = tie(grad_queries, next_a, next_b)
    late_next_a, late_next_b = swap(next_a, "dp", 2), swap(next_b, "dp", 1)

    def one_group(array):
        return jnp.where(group_row == 0, array[:lat_width], array[lat_width:])

    key_part = one_group(contract_rows(latents, grad_keys)).astype(bf16)
    value_part = one_group(contract_rows(latents, grad_values)).astype(bf16)
    one_near, one_far = columns(rows_one, near), columns(rows_one, far)

    def late(left, blocks):
        of_query = contract_rows(left, late_queries)
        of_query = of_query.astype(bf16).reshape(4, block, width)
        return jnp.concatenate([of_query, block_rows(key_part, blocks), block_rows(value_part, blocks)], axis=1)

    late_got = swap(late(one_far, far), "dp", 0)
    ff_parts = finish(rounded_sum(own_a, early_next_a), rounded_sum(own_b, early_next_b))
    lat_next, ff_next = tie(rounded_sum(lat_one, lat_rows(2)), ff_parts[1])
    lat_two = ring(lat_next, -1)
    ff_next = ring(ff_next, 1)
    late_sum = rounded_sum(late(one_near, near), late_got)
    lat_next, late_sum = tie(rounded_sum(lat_two, lat_rows(1)), late_sum)
    lat_three = ring(lat_next, -1)
    late_got = swap(late_sum[2:], "dp", 1)
    grad_latent = rounded_sum(lat_three, lat_rows(0))
    own_a = rounded_sum(keep_a[:, :block], late_a[:, :block])
    own_b = rounded_sum(keep_b[:, :block], late_b[:, :block])

    grad_one = contract_cols(grad_queries, query_full) + contract_cols(grad_latent, latent_down)
    back_one, gain_one = norm_backward(grad_one, normed_one, factor_one, attention_gain)
    tokens_grad = grad_mixed + back_one

    gains = jnp.stack([gain_one, gain_two])

    def last(left, blocks):
        extra = jnp.pad(columns(gains, blocks).T.astype(bf16), ((0, 0), (0, 126)))
        both = jnp.concatenate([contract_rows(left, grad_latent).astype(bf16), extra], axis=1)
        return both.reshape(4, block, both.shape[1])

    last_sum = rounded_sum(last(one_near, near), swap(last(one_far, far), "dp", 0))
    late_sum = rounded_sum(late_sum[:2], late_got)
    ff_parts += finish(rounded_sum(own_a, late_next_a), rounded_sum(own_b, late_next_b))
    ff_next = rounded_sum(ff_next, ff_parts[2])
    last_sum, ff_next, late_sum, out_part = tie(last_sum, ff_next, late_sum, out_part)
    out_grad = plane_sum(ring_columns(out_part)).T
    ff_next = ring(ff_next, 1)
    last_sum = rounded_sum(last_sum[:2], swap(last_sum[2:], "dp", 1))
    late_sum = rounded_sum(late_sum[0], swap(late_sum[1], "dp", 2))
    last_sum = rounded_sum(last_sum[0], swap(last_sum[1], "dp", 2))
    if high > 1:
        cuts = [late_sum[:block], late_sum[block : block + lat_width // 8], late_sum[block + lat_width // 8 :]]
        late_sum = high_bits(jnp.concatenate([cut.reshape(high, -1, width) for cut in cuts], axis=1))
        last_sum = high_bits(last_sum.reshape(high, part, last_sum.shape[1]))
    ff_next = rounded_sum(ff_next, ff_parts[3])
    last_sum, ff_next, late_sum = tie(last_sum, ff_next, late_sum)
    ff_total = ring(ff_next, 1).astype(f32) + ff_parts[0].astype(f32)
    lat_cols = 2 * lat_width // planes

    def last_columns(r):
        return jnp.concatenate(
            [
                lax.dynamic_slice_in_dim(last_sum, (tp ^ r) * lat_cols, lat_cols, 1),
                last_sum[:, 2 * lat_width :],
            ],
            axis=1,
        )

    rows_last, rows_late = part, part + 2 * up_part
    late_columns = ring_columns(late_sum)
    tail = plane_sum(lambda r: jnp.concatenate([last_columns(r), late_columns(r)], axis=0))
    last_sum = tail[:rows_last]
    late_sum = tail[rows_last : rows_last + rows_late]
    query_grad = late_sum[:part]
    key_grad = late_sum[part : part + up_part]
    value_grad = late_sum[part + up_part :]

    ff_mine = ff_total[0]
    ff_other = swap(ff_total[1], "dp", 0)
    ff_first = jnp.where(core == 0, ff_mine, ff_other)
    ff_second = jnp.where(core == 0, ff_other, ff_mine)

    def joined(index):
        lanes = slice(index * ff_pad, index * ff_pad + ff_half)
        return jnp.concatenate([ff_first[:, lanes], ff_second[:, lanes]], axis=1)

    gate_grad, up_grad, down_grad = joined(0), joined(1), joined(2).T
    latent_grad = last_sum[:, :lat_cols]
    return (
        output,
        tokens_grad,
        last_sum[:, lat_cols],
        query_grad,
        latent_grad,
        key_grad,
        value_grad,
        out_grad,
        last_sum[:, lat_cols + 1],
        gate_grad,
        up_grad,
        down_grad,
    )


def solution(mesh):
    return jax.shard_map(
        local,
        mesh=mesh,
        in_specs=(
            P(("dp", "tp"), None),
            P(("dp", "tp"), None),
            P("dp", None),
            P(),
            P(None, "tp"),
            P(),
            P(None, "tp"),
            P(None, "tp"),
            P("tp", None),
            P(),
            P(None, "tp"),
            P(None, "tp"),
            P("tp", None),
        ),
        out_specs=(
            P(("dp", "tp"), None),
            P(("dp", "tp"), None),
            P("dp"),
            P("dp", "tp"),
            P("dp", "tp"),
            P("dp", "tp"),
            P("dp", "tp"),
            P("tp", "dp"),
            P("dp"),
            P("dp", "tp"),
            P("dp", "tp"),
            P("tp", "dp"),
        ),
        check_vma=False,
    )
```

profile of v0, /device:TPU:0, one launch (start us, length us, event | category | flops | bytes accessed | tf_op | source)
XLA Modules:
  0.0 431.0 jit_solution(2161532841944564716)
XLA Ops:
  12.7 3.1 collective-permute-start.2
  22.3 7.5 %collective-permute-done = bf16[128,256]{1,0:T(8,128)(2,1)S(1)} collective-permute-done((bf16[128,256]{1,0:T(8,128)(2,1)S(1)}, bf16[128,256]{1,0:T(8,128)(2,1)S(1)}, u32[]{:S(2)}, u32[]{:S(2)}) %collective-permute-start) | collective-permute-done | bytes 65568 | tf_op jit(solution)/shard_map/ppermute | solution.py:48
  32.1 3.9 collective-permute-done.1
  64.5 7.1 %collective-permute-done.8 = bf16[256,896]{1,0:T(8,128)(2,1)S(1)} collective-permute-done((bf16[256,896]{1,0:T(8,128)(2,1)}, bf16[256,896]{1,0:T(8,128)(2,1)S(1)}, u32[]{:S(2)}, u32[]{:S(2)}) %collective-permute-start.8) | collective-permute-done | bytes 458784 | tf_op jit(solution)/shard_map/ppermute | solution.py:48
  74.1 6.5 %collective-permute-done.9 = bf16[1024,128]{1,0:T(8,128)(2,1)S(1)} collective-permute-done((bf16[1024,128]{1,0:T(8,128)(2,1)S(1)}, bf16[1024,128]{1,0:T(8,128)(2,1)S(1)}, u32[]{:S(2)}, u32[]{:S(2)}) %collective-permute-start.9) | collective-permute-done | bytes 262176 | tf_op jit(solution)/shard_map/ppermute | solution.py:43
  92.5 3.1 collective-permute-done.10
  97.2 3.4 collective-permute-done.18
  110.9 11.9 %collective-permute-done.21 = bf16[128,1152]{1,0:T(8,128)(2,1)S(1)} collective-permute-done((bf16[128,1152]{1,0:T(8,128)(2,1)S(1)}, bf16[128,1152]{1,0:T(8,128)(2,1)S(1)}, u32[]{:S(2)}, u32[]{:S(2)}) %collective-permute-start.21) | collective-permute-done | bytes 294944 | tf_op jit(solution)/shard_map/ppermute | solution.py:43
  130.5 7.3 %collective-permute-done.25 = bf16[256,1152]{1,0:T(8,128)(2,1)S(1)} collective-permute-done((bf16[256,1152]{1,0:T(8,128)(2,1)S(1)}, bf16[256,1152]{1,0:T(8,128)(2,1)S(1)}, u32[]{:S(2)}, u32[]{:S(2)}) %collective-permute-start.25) | collective-permute-done | bytes 589856 | tf_op jit(solution)/shard_map/ppermute | solution.py:48
  142.4 3.2 copy.37
  145.6 8.7 %attend_forward.3 = (bf16[256,512]{1,0:T(8,128)(2,1)}, bf16[8,256,1024]{2,1,0:T(8,128)(2,1)}) custom-call(s32[5]{0:T(128)} %stack.287.info, bf16[256,1024]{1,0:T(8,128)(2,1)} %convolution_convert_fusion.8.q_ref, bf16[1024,1024]{1,0:T(8,128)(2,1)} %convolution_convert_fusion.2.k_ref, bf16[1024,1024]{1,0:T(8,128)(2,1)} %convolution_convert_fusion.1.v_ref), custom_call_target="tpu_custom_call" | custom-call | tf_op jit(solution)/shard_map/attend_forward/pallas_call | solution.py:128
  154.3 8.7 %attend_forward.2 = (bf16[256,512]{1,0:T(8,128)(2,1)}, bf16[8,256,1024]{2,1,0:T(8,128)(2,1)}) custom-call(s32[5]{0:T(128)} %stack.287.info, bf16[256,1024]{1,0:T(8,128)(2,1)} %convolution_convert_fusion.8.q_ref, bf16[1024,1024]{1,0:T(8,128)(2,1)} %convolution_convert_fusion.2.k_ref, bf16[1024,1024]{1,0:T(8,128)(2,1)} %convolution_convert_fusion.1.v_ref), custom_call_target="tpu_custom_call" | custom-call | tf_op jit(solution)/shard_map/attend_forward/pallas_call | solution.py:128
  177.4 13.6 %feed_forward.2 = (bf16[2,512,768]{2,1,0:T(8,128)(2,1)}, bf16[2,512,384]{2,1,0:T(8,128)(2,1)}, f32[512,1024]{1,0:T(8,128)}, f32[512,1024]{1,0:T(8,128)}, bf16[10...) custom-call(bf16[512,1024]{1,0:T(8,128)(2,1)} %pad_maximum_fusion.13.refs_0_, ...), custom_call_target="tpu_custom_call" | custom-call | tf_op jit(solution)/shard_map/feed_forward/pallas_call | solution.py:222
  191.1 5.0 %feed_grads.4 = (bf16[2,256,1152]{2,1,0:T(8,128)(2,1)}, bf16[2,256,1152]{2,1,0:T(8,128)(2,1)}) custom-call(s32[4]{0:T(128)} %pad_add_fusion.1.spots, bf16[1024,512]{1,0:T(8,128)(2,1)} %get-tuple-element.91.refs_0_.refs_1_.refs_2_.refs_3_, bf16[1024,512]{1,0:T(8,128)(2,1)} %get-tuple-element.91.refs_0_.refs_1_.refs_2_.refs_3_, ...), custom_call_target="tpu_custom_call" | custom-call | tf_op jit(solution)/shard_map/feed_grads/pallas_call | solution.py:264
  204.0 14.5 %feed_forward.3 = (bf16[2,512,768]{2,1,0:T(8,128)(2,1)}, bf16[2,512,384]{2,1,0:T(8,128)(2,1)}, f32[512,1024]{1,0:T(8,128)}, f32[512,1024]{1,0:T(8,128)}, bf16[25...) custom-call(bf16[512,1024]{1,0:T(8,128)(2,1)} %pad_maximum_fusion.13.refs_0_, ...), custom_call_target="tpu_custom_call" | custom-call | tf_op jit(solution)/shard_map/feed_forward/pallas_call | solution.py:222
  223.5 5.0 %feed_grads.5 = (bf16[2,256,1152]{2,1,0:T(8,128)(2,1)}, bf16[2,256,1152]{2,1,0:T(8,128)(2,1)}) custom-call(s32[4]{0:T(128)} %pad_add_fusion.1.spots, bf16[1024,512]{1,0:T(8,128)(2,1)} %get-tuple-element.91.refs_0_.refs_1_.refs_2_.refs_3_, bf16[1024,512]{1,0:T(8,128)(2,1)} %get-tuple-element.91.refs_0_.refs_1_.refs_2_.refs_3_, ...), custom_call_target="tpu_custom_call" | custom-call | tf_op jit(solution)/shard_map/feed_grads/pallas_call | solution.py:264
  232.8 3.3 multiply_add_fusion
  237.7 9.5 %attend_backward.2 = (bf16[256,512]{1,0:T(8,128)(2,1)}, bf16[1024,512]{1,0:T(8,128)(2,1)}, bf16[1024,512]{1,0:T(8,128)(2,1)}) custom-call(bf16[256,1024]{1,0:T(8,128)(2,1)} %convolution_convert_fusion.8.q_ref, bf16[1024,1024]{1,0:T(8,128)(2,1)} %convolution_convert_fusion.2.k_ref, bf16[1024,1024]{1,0:T(8,128)(2,1)} %convolution_convert_fusion.1.v_ref, ...), custom_call_target="tpu_custom_call" | custom-call | tf_op jit(solution)/shard_map/attend_backward/pallas_call | solution.py:155
  249.4 5.1 %feed_grads.6 = (bf16[2,256,1152]{2,1,0:T(8,128)(2,1)}, bf16[2,256,1152]{2,1,0:T(8,128)(2,1)}) custom-call(s32[4]{0:T(128)} %pad_add_fusion.2.spots, bf16[1024,512]{1,0:T(8,128)(2,1)} %get-tuple-element.91.refs_0_.refs_1_.refs_2_.refs_3_, bf16[1024,512]{1,0:T(8,128)(2,1)} %get-tuple-element.91.refs_0_.refs_1_.refs_2_.refs_3_, ...), custom_call_target="tpu_custom_call" | custom-call | tf_op jit(solution)/shard_map/feed_grads/pallas_call | solution.py:264
  261.5 9.5 %attend_backward.3 = (bf16[256,512]{1,0:T(8,128)(2,1)}, bf16[1024,512]{1,0:T(8,128)(2,1)}, bf16[1024,512]{1,0:T(8,128)(2,1)}) custom-call(bf16[256,1024]{1,0:T(8,128)(2,1)} %convolution_convert_fusion.8.q_ref, bf16[1024,1024]{1,0:T(8,128)(2,1)} %convolution_convert_fusion.2.k_ref, bf16[1024,1024]{1,0:T(8,128)(2,1)} %convolution_convert_fusion.1.v_ref, ...), custom_call_target="tpu_custom_call" | custom-call | tf_op jit(solution)/shard_map/attend_backward/pallas_call | solution.py:155
  273.4 3.0 fusion.22
  280.2 5.2 %feed_grads.7 = (bf16[2,256,1152]{2,1,0:T(8,128)(2,1)}, bf16[2,256,1152]{2,1,0:T(8,128)(2,1)}) custom-call(s32[4]{0:T(128)} %pad_add_fusion.2.spots, bf16[1024,512]{1,0:T(8,128)(2,1)} %get-tuple-element.91.refs_0_.refs_1_.refs_2_.refs_3_, bf16[1024,512]{1,0:T(8,128)(2,1)} %get-tuple-element.91.refs_0_.refs_1_.refs_2_.refs_3_, ...), custom_call_target="tpu_custom_call" | custom-call | tf_op jit(solution)/shard_map/feed_grads/pallas_call | solution.py:264
  286.4 3.3 fusion.60
  303.3 4.5 %collective-permute-done.34 = bf16[256,512]{1,0:T(8,128)(2,1)S(1)} collective-permute-done((bf16[256,512]{1,0:T(8,128)(2,1)S(1)}, bf16[256,512]{1,0:T(8,128)(2,1)S(1)}, u32[]{:S(2)}, u32[]{:S(2)}) %collective-permute-start.34) | collective-permute-done | bytes 262176 | tf_op jit(solution)/shard_map/ppermute | solution.py:48
  318.0 3.8 collective-permute-done.44
  331.2 6.6 %collective-permute-done.43 = bf16[2,128,1152]{2,1,0:T(8,128)(2,1)S(1)} collective-permute-done((bf16[2,128,1152]{2,1,0:T(8,128)(2,1)S(1)}, bf16[2,128,1152]{2,1,0:T(8,128)(2,1)S(1)}, u32[]{:S(2)}, u32[]{:S(2)}) %collective-permute-start.43) | collective-permute-done | bytes 589856 | tf_op jit(solution)/shard_map/ppermute | solution.py:48
  352.0 4.5 %collective-permute-done.46 = bf16[2,192,1024]{2,1,0:T(8,128)(2,1)} collective-permute-done((bf16[2,192,1024]{2,1,0:T(8,128)(2,1)}, bf16[2,192,1024]{2,1,0:T(8,128)(2,1)}, u32[]{:S(2)}, u32[]{:S(2)}) %collective-permute-start.46) | collective-permute-done | bytes 786464 | tf_op jit(solution)/shard_map/ppermute | solution.py:43
  374.5 6.3 %collective-permute-done.49 = bf16[2,128,1152]{2,1,0:T(8,128)(2,1)S(1)} collective-permute-done((bf16[2,128,1152]{2,1,0:T(8,128)(2,1)}, bf16[2,128,1152]{2,1,0:T(8,128)(2,1)S(1)}, u32[]{:S(2)}, u32[]{:S(2)}) %collective-permute-start.49) | collective-permute-done | bytes 589856 | tf_op jit(solution)/shard_map/ppermute | solution.py:48
  381.0 2.9 collective-permute-start.55
  388.5 14.2 %collective-permute-done.53 = bf16[128,512]{1,0:T(8,128)(2,1)S(1)} collective-permute-done((bf16[128,512]{1,0:T(8,128)(2,1)S(1)}, bf16[128,512]{1,0:T(8,128)(2,1)S(1)}, u32[]{:S(2)}, u32[]{:S(2)}) %collective-permute-start.53) | collective-permute-done | bytes 131104 | tf_op jit(solution)/shard_map/ppermute | solution.py:43
  402.7 6.9 %collective-permute-done.51 = bf16[320,512]{1,0:T(8,128)(2,1)S(1)} collective-permute-done((bf16[320,512]{1,0:T(8,128)(2,1)S(1)}, bf16[320,512]{1,0:T(8,128)(2,1)S(1)}, u32[]{:S(2)}, u32[]{:S(2)}) %collective-permute-start.51) | collective-permute-done | bytes 327712 | tf_op jit(solution)/shard_map/ppermute | solution.py:43
  411.8 5.1 %collective-permute-done.52 = bf16[320,256]{1,0:T(8,128)(2,1)} collective-permute-done((bf16[320,256]{1,0:T(8,128)(2,1)}, bf16[320,256]{1,0:T(8,128)(2,1)}, u32[]{:S(2)}, u32[]{:S(2)}) %collective-permute-start.52) | collective-permute-done | bytes 163872 | tf_op jit(solution)/shard_map/ppermute | solution.py:43
  (453 shorter events, 208.5 us)
Async XLA Ops:
  7.2 353.0 %reduce-scatter.2.cloned.1.call-start = ((), (), s32[]{:S(2)}) async-start(), calls=%async_computation.1 | async-start | bytes 2359296 | tf_op jit(solution)/shard_map/reduce_scatter | solution.py:493
  12.7 23.2 %collective-permute-start.2 = (bf16[256,896]{1,0:T(8,128)(2,1)S(1)}, bf16[256,896]{1,0:T(8,128)(2,1)}, u32[]{:S(2)}, u32[]{:S(2)}) collective-permute-start(bf16[256,896]{1,0:T(8,128)(2,1)S(1)} %pad_maximum_fusion.29), channel_id=1, source_target_pairs={{0,1},{1,2},{2,3},{3,0},{4,5},{5,6},{6,7},{7,4},{8,9},{9,10},{10,1... | collective-permute-start | bytes 1376264 | tf_op jit(solution)/shard_map/ppermute | solution.py:48
  18.3 31.6 %collective-permute-start.14 = (bf16[256,1024]{1,0:T(8,128)(2,1)}, bf16[256,1024]{1,0:T(8,128)(2,1)}, u32[]{:S(2)}, u32[]{:S(2)}) collective-permute-start(bf16[256,1024]{1,0:T(8,128)(2,1)} %param.14), channel_id=1, source_target_pairs={{0,4},{4,0},{8,12},{12,8},{16,20},{20,16},{24,28},{28,24},{1,5},{5... | collective-permute-start | bytes 1572872 | tf_op jit(solution)/shard_map/ppermute | solution.py:43
  36.3 17.6 %collective-permute-start.5 = (bf16[256,896]{1,0:T(8,128)(2,1)}, bf16[256,896]{1,0:T(8,128)(2,1)}, u32[]{:S(2)}, u32[]{:S(2)}) collective-permute-start(bf16[256,896]{1,0:T(8,128)(2,1)} %collective-permute-done.2), channel_id=1, source_target_pairs={{0,1},{1,2},{2,3},{3,0},{4,5},{5,6},{6,7},{7,4},{8,9},{9,10},{10,1... | collective-permute-start | bytes 1376264 | tf_op jit(solution)/shard_map/ppermute | solution.py:48
  71.6 17.2 %collective-permute-start.15 = (bf16[256,1152]{1,0:T(8,128)(2,1)S(1)}, bf16[256,1152]{1,0:T(8,128)(2,1)S(1)}, u32[]{:S(2)}, u32[]{:S(2)}) collective-permute-start(bf16[256,1152]{1,0:T(8,128)(2,1)S(1)} %pad_maximum_fusion.18), channel_id=1, source_target_pairs={{0,1},{1,2},{2,3},{3,0},{4,5},{5,6},{6,7},{7,4},{8,9},{9,10},{10,1... | collective-permute-start | bytes 1769480 | tf_op jit(solution)/shard_map/ppermute | solution.py:48
  73.8 30.4 %collective-permute-start.7 = (bf16[2,2,4,128,256]{4,3,2,1,0:T(8,128)(2,1)S(1)}, bf16[2,2,4,128,256]{4,3,2,1,0:T(8,128)(2,1)S(1)}, u32[]{:S(2)}, u32[]{:S(2)}) collective-permute-start(bf16[2,2,4,128,256]{4,3,2,1,0:T(8,128)(2,1)S(1)} %pad_maximum_fusion.8), channel_id=1, source_target_pairs={{0,4},{4,0},{8,12},{12,8},{16,20},{20,16},{24,28},{28,24},{1,5},{5... | collective-permute-start | bytes 3145736 | tf_op jit(solution)/shard_map/ppermute | solution.py:43
  90.9 16.2 %collective-permute-start.20 = (bf16[256,1152]{1,0:T(8,128)(2,1)S(1)}, bf16[256,1152]{1,0:T(8,128)(2,1)S(1)}, u32[]{:S(2)}, u32[]{:S(2)}) collective-permute-start(bf16[256,1152]{1,0:T(8,128)(2,1)S(1)} %collective-permute-done.15), channel_id=1, source_target_pairs={{0,1},{1,2},{2,3},{3,0},{4,5},{5,6},{6,7},{7,4},{8,9},{9,10},{10,1... | collective-permute-start | bytes 1769480 | tf_op jit(solution)/shard_map/ppermute | solution.py:48
  95.8 44.9 %collective-permute-start.11 = (bf16[2,2,1024,128]{3,2,1,0:T(8,128)(2,1)S(1)}, bf16[2,2,1024,128]{3,2,1,0:T(8,128)(2,1)S(1)}, u32[]{:S(2)}, u32[]{:S(2)}) collective-permute-start(bf16[2,2,1024,128]{3,2,1,0:T(8,128)(2,1)S(1)} %pad_maximum_fusion.9), channel_id=1, source_target_pairs={{0,4},{4,0},{8,12},{12,8},{16,20},{20,16},{24,28},{28,24},{1,5},{5... | collective-permute-start | bytes 3145736 | tf_op jit(solution)/shard_map/ppermute | solution.py:43
  100.8 26.0 %collective-permute-start.17 = (bf16[2,128,1152]{2,1,0:T(8,128)(2,1)S(1)}, bf16[2,128,1152]{2,1,0:T(8,128)(2,1)S(1)}, u32[]{:S(2)}, u32[]{:S(2)}) collective-permute-start(bf16[2,128,1152]{2,1,0:T(8,128)(2,1)S(1)} %pad_maximum_fusion.19), channel_id=1, source_target_pairs={{0,16},{4,20},{8,24},{12,28},{16,0},{20,4},{24,8},{28,12},{1,17},{... | collective-permute-start | bytes 1769480 | tf_op jit(solution)/shard_map/ppermute | solution.py:43
  102.7 25.7 %collective-permute-start.19 = (bf16[2,128,1152]{2,1,0:T(8,128)(2,1)S(1)}, bf16[2,128,1152]{2,1,0:T(8,128)(2,1)S(1)}, u32[]{:S(2)}, u32[]{:S(2)}) collective-permute-start(bf16[2,128,1152]{2,1,0:T(8,128)(2,1)S(1)} %pad_maximum_fusion.20), channel_id=1, source_target_pairs={{0,8},{4,12},{8,0},{12,4},{16,24},{20,28},{24,16},{28,20},{1,9},{5... | collective-permute-start | bytes 1769480 | tf_op jit(solution)/shard_map/ppermute | solution.py:43
  107.7 16.5 %collective-permute-start.23 = (bf16[128,1152]{1,0:T(8,128)(2,1)S(1)}, bf16[128,1152]{1,0:T(8,128)(2,1)S(1)}, u32[]{:S(2)}, u32[]{:S(2)}) collective-permute-start(bf16[128,1152]{1,0:T(8,128)(2,1)S(1)} %get-tuple-element.235), channel_id=1, source_target_pairs={{0,16},{4,20},{8,24},{12,28},{16,0},{20,4},{24,8},{28,12},{1,17},{... | collective-permute-start | bytes 884744 | tf_op jit(solution)/shard_map/ppermute | solution.py:43
  125.4 70.7 %collective-permute-start.22 = (bf16[2,128,1152]{2,1,0:T(8,128)(2,1)}, bf16[2,128,1152]{2,1,0:T(8,128)(2,1)}, u32[]{:S(2)}, u32[]{:S(2)}) collective-permute-start(bf16[2,128,1152]{2,1,0:T(8,128)(2,1)} %pad_maximum_fusion.21), channel_id=1, source_target_pairs={{0,16},{4,20},{8,24},{12,28},{16,0},{20,4},{24,8},{28,12},{1,17},{... | collective-permute-start | bytes 1769480 | tf_op jit(solution)/shard_map/ppermute | solution.py:43
  126.8 71.3 %collective-permute-start.24 = (bf16[2,128,1152]{2,1,0:T(8,128)(2,1)}, bf16[2,128,1152]{2,1,0:T(8,128)(2,1)}, u32[]{:S(2)}, u32[]{:S(2)}) collective-permute-start(bf16[2,128,1152]{2,1,0:T(8,128)(2,1)} %pad_maximum_fusion.22), channel_id=1, source_target_pairs={{0,8},{4,12},{8,0},{12,4},{16,24},{20,28},{24,16},{28,20},{1,9},{5... | collective-permute-start | bytes 1769480 | tf_op jit(solution)/shard_map/ppermute | solution.py:43
  138.7 28.8 %collective-permute-start.26 = (bf16[128,1152]{1,0:T(8,128)(2,1)}, bf16[128,1152]{1,0:T(8,128)(2,1)}, u32[]{:S(2)}, u32[]{:S(2)}) collective-permute-start(bf16[128,1152]{1,0:T(8,128)(2,1)} %get-tuple-element.238), channel_id=1, source_target_pairs={{0,8},{4,12},{8,0},{12,4},{16,24},{20,28},{24,16},{28,20},{1,9},{5... | collective-permute-start | bytes 884744 | tf_op jit(solution)/shard_map/ppermute | solution.py:43
  140.2 27.3 %collective-permute-start.28 = (bf16[128,1152]{1,0:T(8,128)(2,1)}, bf16[128,1152]{1,0:T(8,128)(2,1)}, u32[]{:S(2)}, u32[]{:S(2)}) collective-permute-start(bf16[128,1152]{1,0:T(8,128)(2,1)} %get-tuple-element.239), channel_id=1, source_target_pairs={{0,16},{4,20},{8,24},{12,28},{16,0},{20,4},{24,8},{28,12},{1,17},{... | collective-permute-start | bytes 884744 | tf_op jit(solution)/shard_map/ppermute | solution.py:43
  170.8 25.3 %collective-permute-start.27 = (bf16[2,128,1152]{2,1,0:T(8,128)(2,1)}, bf16[2,128,1152]{2,1,0:T(8,128)(2,1)}, u32[]{:S(2)}, u32[]{:S(2)}) collective-permute-start(bf16[2,128,1152]{2,1,0:T(8,128)(2,1)} %pad_maximum_fusion.23), channel_id=1, source_target_pairs={{0,16},{4,20},{8,24},{12,28},{16,0},{20,4},{24,8},{28,12},{1,17},{... | collective-permute-start | bytes 1769480 | tf_op jit(solution)/shard_map/ppermute | solution.py:43
  175.8 22.2 %collective-permute-start.29 = (bf16[2,128,1152]{2,1,0:T(8,128)(2,1)}, bf16[2,128,1152]{2,1,0:T(8,128)(2,1)}, u32[]{:S(2)}, u32[]{:S(2)}) collective-permute-start(bf16[2,128,1152]{2,1,0:T(8,128)(2,1)} %pad_maximum_fusion.24), channel_id=1, source_target_pairs={{0,8},{4,12},{8,0},{12,4},{16,24},{20,28},{24,16},{28,20},{1,9},{5... | collective-permute-start | bytes 1769480 | tf_op jit(solution)/shard_map/ppermute | solution.py:43
  221.5 36.7 %collective-permute-start.33 = (bf16[2,256,1152]{2,1,0:T(8,128)(2,1)}, bf16[2,256,1152]{2,1,0:T(8,128)(2,1)}, u32[]{:S(2)}, u32[]{:S(2)}) collective-permute-start(bf16[2,256,1152]{2,1,0:T(8,128)(2,1)} %get-tuple-element.117), channel_id=1, source_target_pairs={{0,16},{4,20},{8,24},{12,28},{16,0},{20,4},{24,8},{28,12},{1,17},{... | collective-permute-start | bytes 3538952 | tf_op jit(solution)/shard_map/ppermute | solution.py:43
  221.8 37.6 %collective-permute-start.32 = (bf16[2,256,1152]{2,1,0:T(8,128)(2,1)}, bf16[2,256,1152]{2,1,0:T(8,128)(2,1)}, u32[]{:S(2)}, u32[]{:S(2)}) collective-permute-start(bf16[2,256,1152]{2,1,0:T(8,128)(2,1)} %get-tuple-element.115), channel_id=1, source_target_pairs={{0,8},{4,12},{8,0},{12,4},{16,24},{20,28},{24,16},{28,20},{1,9},{5... | collective-permute-start | bytes 3538952 | tf_op jit(solution)/shard_map/ppermute | solution.py:43
  228.5 62.6 %collective-permute-start.39 = (bf16[2,256,1152]{2,1,0:T(8,128)(2,1)}, bf16[2,256,1152]{2,1,0:T(8,128)(2,1)}, u32[]{:S(2)}, u32[]{:S(2)}) collective-permute-start(bf16[2,256,1152]{2,1,0:T(8,128)(2,1)} %get-tuple-element.107), channel_id=1, source_target_pairs={{0,16},{4,20},{8,24},{12,28},{16,0},{20,4},{24,8},{28,12},{1,17},{... | collective-permute-start | bytes 3538952 | tf_op jit(solution)/shard_map/ppermute | solution.py:43
  230.1 62.3 %collective-permute-start.38 = (bf16[2,256,1152]{2,1,0:T(8,128)(2,1)}, bf16[2,256,1152]{2,1,0:T(8,128)(2,1)}, u32[]{:S(2)}, u32[]{:S(2)}) collective-permute-start(bf16[2,256,1152]{2,1,0:T(8,128)(2,1)} %get-tuple-element.106), channel_id=1, source_target_pairs={{0,8},{4,12},{8,0},{12,4},{16,24},{20,28},{24,16},{28,20},{1,9},{5... | collective-permute-start | bytes 3538952 | tf_op jit(solution)/shard_map/ppermute | solution.py:43
  294.8 16.2 %collective-permute-start.35 = (bf16[2,128,1152]{2,1,0:T(8,128)(2,1)S(1)}, bf16[2,128,1152]{2,1,0:T(8,128)(2,1)S(1)}, u32[]{:S(2)}, u32[]{:S(2)}) collective-permute-start(bf16[2,128,1152]{2,1,0:T(8,128)(2,1)S(1)} %copy-done.48), channel_id=1, source_target_pairs={{0,16},{4,20},{8,24},{12,28},{16,0},{20,4},{24,8},{28,12},{1,17},{... | collective-permute-start | bytes 1769480 | tf_op jit(solution)/shard_map/ppermute | solution.py:43
  297.5 30.6 %collective-permute-start.40 = (bf16[4,192,1024]{2,1,0:T(8,128)(2,1)S(1)}, bf16[4,192,1024]{2,1,0:T(8,128)(2,1)S(1)}, u32[]{:S(2)}, u32[]{:S(2)}) collective-permute-start(bf16[4,192,1024]{2,1,0:T(8,128)(2,1)S(1)} %maximum_maximum_fusion), channel_id=1, source_target_pairs={{0,4},{4,0},{8,12},{12,8},{16,20},{20,16},{24,28},{28,24},{1,5},{5... | collective-permute-start | bytes 4718600 | tf_op jit(solution)/shard_map/ppermute | solution.py:43
  297.6 16.3 %collective-permute-start.36 = (bf16[2,128,1152]{2,1,0:T(8,128)(2,1)S(1)}, bf16[2,128,1152]{2,1,0:T(8,128)(2,1)S(1)}, u32[]{:S(2)}, u32[]{:S(2)}) collective-permute-start(bf16[2,128,1152]{2,1,0:T(8,128)(2,1)S(1)} %add_convert_fusion.16), channel_id=1, source_target_pairs={{0,8},{4,12},{8,0},{12,4},{16,24},{20,28},{24,16},{28,20},{1,9},{5... | collective-permute-start | bytes 1769480 | tf_op jit(solution)/shard_map/ppermute | solution.py:43
  301.4 20.4 %collective-permute-start.44 = (bf16[2,128,1152]{2,1,0:T(8,128)(2,1)S(1)}, bf16[2,128,1152]{2,1,0:T(8,128)(2,1)S(1)}, u32[]{:S(2)}, u32[]{:S(2)}) collective-permute-start(bf16[2,128,1152]{2,1,0:T(8,128)(2,1)S(1)} %add_convert_fusion.11), channel_id=1, source_target_pairs={{0,16},{4,20},{8,24},{12,28},{16,0},{20,4},{24,8},{28,12},{1,17},{... | collective-permute-start | bytes 1769480 | tf_op jit(solution)/shard_map/ppermute | solution.py:43
  307.8 18.2 %collective-permute-start.45 = (bf16[2,128,1152]{2,1,0:T(8,128)(2,1)S(1)}, bf16[2,128,1152]{2,1,0:T(8,128)(2,1)S(1)}, u32[]{:S(2)}, u32[]{:S(2)}) collective-permute-start(bf16[2,128,1152]{2,1,0:T(8,128)(2,1)S(1)} %add_convert_fusion.10), channel_id=1, source_target_pairs={{0,8},{4,12},{8,0},{12,4},{16,24},{20,28},{24,16},{28,20},{1,9},{5... | collective-permute-start | bytes 1769480 | tf_op jit(solution)/shard_map/ppermute | solution.py:43
  318.0 19.8 %collective-permute-start.43 = (bf16[2,128,1152]{2,1,0:T(8,128)(2,1)S(1)}, bf16[2,128,1152]{2,1,0:T(8,128)(2,1)S(1)}, u32[]{:S(2)}, u32[]{:S(2)}) collective-permute-start(bf16[2,128,1152]{2,1,0:T(8,128)(2,1)S(1)} %pad_maximum_fusion.25), channel_id=1, source_target_pairs={{0,1},{1,2},{2,3},{3,0},{4,5},{5,6},{6,7},{7,4},{8,9},{9,10},{10,1... | collective-permute-start | bytes 1769480 | tf_op jit(solution)/shard_map/ppermute | solution.py:48
  339.8 16.6 %collective-permute-start.46 = (bf16[2,192,1024]{2,1,0:T(8,128)(2,1)}, bf16[2,192,1024]{2,1,0:T(8,128)(2,1)}, u32[]{:S(2)}, u32[]{:S(2)}) collective-permute-start(bf16[2,192,1024]{2,1,0:T(8,128)(2,1)} %slice.307), channel_id=1, source_target_pairs={{0,8},{4,12},{8,0},{12,4},{16,24},{20,28},{24,16},{28,20},{1,9},{5... | collective-permute-start | bytes 2359304 | tf_op jit(solution)/shard_map/ppermute | solution.py:43
  364.5 16.4 %collective-permute-start.49 = (bf16[2,128,1152]{2,1,0:T(8,128)(2,1)}, bf16[2,128,1152]{2,1,0:T(8,128)(2,1)S(1)}, u32[]{:S(2)}, u32[]{:S(2)}) collective-permute-start(bf16[2,128,1152]{2,1,0:T(8,128)(2,1)} %add_convert_fusion.5), channel_id=1, source_target_pairs={{0,1},{1,2},{2,3},{3,0},{4,5},{5,6},{6,7},{7,4},{8,9},{9,10},{10,1... | collective-permute-start | bytes 1769480 | tf_op jit(solution)/shard_map/ppermute | solution.py:48
  366.9 35.7 %collective-permute-start.53 = (bf16[128,512]{1,0:T(8,128)(2,1)S(1)}, bf16[128,512]{1,0:T(8,128)(2,1)S(1)}, u32[]{:S(2)}, u32[]{:S(2)}) collective-permute-start(bf16[128,512]{1,0:T(8,128)(2,1)S(1)} %pad_maximum_fusion.38), channel_id=1, source_target_pairs={{0,2},{1,3},{2,0},{3,1},{4,6},{5,7},{6,4},{7,5},{8,10},{9,11},{10,... | collective-permute-start | bytes 393224 | tf_op jit(solution)/shard_map/ppermute | solution.py:43
  381.0 29.4 %collective-permute-start.55 = (bf16[2,128,1152]{2,1,0:T(8,128)(2,1)S(1)}, bf16[2,128,1152]{2,1,0:T(8,128)(2,1)S(1)}, u32[]{:S(2)}, u32[]{:S(2)}) collective-permute-start(bf16[2,128,1152]{2,1,0:T(8,128)(2,1)S(1)} %add_convert_fusion.4), channel_id=1, source_target_pairs={{0,1},{1,2},{2,3},{3,0},{4,5},{5,6},{6,7},{7,4},{8,9},{9,10},{10,1... | collective-permute-start | bytes 1769480 | tf_op jit(solution)/shard_map/ppermute | solution.py:48
  385.3 24.4 %collective-permute-start.51 = (bf16[320,512]{1,0:T(8,128)(2,1)S(1)}, bf16[320,512]{1,0:T(8,128)(2,1)S(1)}, u32[]{:S(2)}, u32[]{:S(2)}) collective-permute-start(bf16[320,512]{1,0:T(8,128)(2,1)S(1)} %maximum_maximum_fusion.1), channel_id=1, source_target_pairs={{0,2},{1,3},{2,0},{3,1},{4,6},{5,7},{6,4},{7,5},{8,10},{9,11},{10,... | collective-permute-start | bytes 983048 | tf_op jit(solution)/shard_map/ppermute | solution.py:43
  (114 other events, 859.2 us)
Sparse Core Ops, SparseCore 0:
  249.5 43.2 reduce-scatter.1
where the time goes:
time: 439 us; the launch traced here: 431 us
  waiting for transfers between devices  119 us (27%)
  Pallas kernels  84.9 us (19%)
  local copies, waits for them, and re-layouts  64.8 us (15%)
  other arithmetic  60.8 us (14%)
  starting transfers between devices  57.1 us (13%)
  matrix products  27.9 us (6%)
  between operations  16.1 us (4%)
    ppermute x42, waiting for transfers between devices, swap(): return lax.ppermute(block, axis, [(i, i ^ 1 << bit) for i in range(count)])  72.7 us
    ppermute x15, waiting for transfers between devices, ring(): lax.ppermute(block, 'tp', [(i, (i + step) % count) for i in range(count)])  46.6 us
    ppermute x42, starting transfers between devices, swap(): return lax.ppermute(block, axis, [(i, i ^ 1 << bit) for i in range(count)])  38.5 us
    pallas_call x2, Pallas kernels, feed_forward(): pl.pallas_call(functools.partial(feed_kernel, len(starts) > 0, with_send)...  28.1 us
    pallas_call x4, Pallas kernels, feed_grads(): pl.pallas_call(feed_grad_kernel, grid_spec=pltpu.PrefetchScalarGridSpec(n...  20.4 us
    pallas_call x2, Pallas kernels, attend_backward(): pl.pallas_call(backward_kernel, grid=(pairs,), in_specs=[part, deep, deep...  19 us
    ppermute x15, starting transfers between devices, ring(): lax.ppermute(block, 'tp', [(i, (i + step) % count) for i in range(count)])  18.5 us
    convert_element_type x19, other arithmetic, rounded_sum(): return (left.astype(f32) + right.astype(f32)).astype(bf16)  18.3 us
  transfers between devices with their start and end apart: 58, of which 28 were waited for; matrix products, arithmetic and copies ran while one was open for 30% of the time, Pallas kernels for 16%

commit v1 on v0

--- a/solution.py
+++ b/solution.py
@@ -73,7 +73,8 @@
     return rounded_sum(keep, swap(send, "dp", bit))
 
 
-def forward_kernel(info, q_ref, k_ref, v_ref, o_ref, w_ref, bias_ref):
+def forward_kernel(info, q_ref, k_ref, v_ref, *refs):
+    o_ref, w_ref, bias_ref = refs[-3:]
     rows, keys = bias_ref.shape
 
     @pl.when(pl.program_id(0) == 0)
@@ -98,7 +99,8 @@
     o_ref[...] = jnp.concatenate(outs, axis=1)
 
 
-def backward_kernel(q_ref, k_ref, v_ref, g_ref, w_ref, dq_ref, dk_ref, dv_ref):
+def backward_kernel(q_ref, k_ref, v_ref, g_ref, w_ref, *refs):
+    dq_ref, dk_ref, dv_ref = refs[-3:]
     dqs, dks, dvs = [], [], []
     for j in range(2):
         lanes = slice(j * HD, (j + 1) * HD)
@@ -116,13 +118,11 @@
     dv_ref[...] = jnp.concatenate(dvs, axis=1)
 
 
-def attend_forward(queries, keys, values, info, half):
+def attend_forward(queries, keys, values, info, half, *started):
     rows, width = queries.shape
     total = keys.shape[0]
     pairs = width // (4 * HD)
-    width = width // 2
     skip = half * pairs
-    small = pl.BlockSpec((rows, 2 * HD), lambda h, s: (0, h))
     part = pl.BlockSpec((rows, 2 * HD), lambda h, s: (0, skip + h))
     large = pl.BlockSpec((total, 2 * HD), lambda h, s: (0, skip + h))
     return pl.pallas_call(
@@ -130,40 +130,40 @@
         grid_spec=pltpu.PrefetchScalarGridSpec(
             num_scalar_prefetch=1,
             grid=(pairs,),
-            in_specs=[part, large, large],
-            out_specs=[small, pl.BlockSpec((2, rows, total), lambda h, s: (h, 0, 0))],
+            in_specs=[part, large, large] + [pl.BlockSpec(memory_space=pl.ANY)] * len(started),
+            out_specs=[part, pl.BlockSpec((2, rows, total), lambda h, s: (h, 0, 0))],
             scratch_shapes=[pltpu.VMEM((rows, total), f32)],
         ),
         out_shape=[
             jax.ShapeDtypeStruct((rows, width), bf16),
             jax.ShapeDtypeStruct((2 * pairs, rows, total), bf16),
         ],
+        input_output_aliases={4: 0} if started else {},
         name="attend_forward",
-    )(info, queries, keys, values)
-
-
-def attend_backward(queries, keys, values, grad, weights, half):
+    )(info, queries, keys, values, *started)
+
+
+def attend_backward(queries, keys, values, grad, weights, half, *started):
     rows, width = queries.shape
     total = keys.shape[0]
     pairs = width // (4 * HD)
-    width = width // 2
     skip = half * pairs
-    small = pl.BlockSpec((rows, 2 * HD), lambda h: (0, h))
-    large = pl.BlockSpec((total, 2 * HD), lambda h: (0, h))
     part = pl.BlockSpec((rows, 2 * HD), lambda h: (0, skip + h))
     deep = pl.BlockSpec((total, 2 * HD), lambda h: (0, skip + h))
     return pl.pallas_call(
         backward_kernel,
         grid=(pairs,),
-        in_specs=[part, deep, deep, part, pl.BlockSpec((2, rows, total), lambda h: (h, 0, 0))],
-        out_specs=[small, large, large],
+        in_specs=[part, deep, deep, part, pl.BlockSpec((2, rows, total), lambda h: (h, 0, 0))]
+        + [pl.BlockSpec(memory_space=pl.ANY)] * len(started),
+        out_specs=[part, deep, deep],
         out_shape=[
             jax.ShapeDtypeStruct((rows, width), bf16),
             jax.ShapeDtypeStruct((total, width), bf16),
             jax.ShapeDtypeStruct((total, width), bf16),
         ],
+        input_output_aliases={5: 0, 6: 1, 7: 2} if started else {},
         name="attend_backward",
-    )(queries, keys, values, grad, weights)
+    )(queries, keys, values, grad, weights, *started)
 
 
 def feed_kernel(with_start, with_send, *refs):
@@ -335,18 +335,18 @@
     latent_own = matmul(rows_one, latent_down).astype(bf16)
     up_piece = jnp.where(core == 0, key_up, value_up)
     o_piece = lax.dynamic_slice_in_dim(out_weight, eighth * block, block, 1)
-    lat_up = jnp.concatenate([latent_own, up_piece, o_piece], axis=1)
-    q_list, lat_got = [q_piece], [lat_up]
-    q_list.append(ring(q_piece, 1))
-    lat_got.append(ring(lat_up, 1))
-    q_list.append(ring(q_list[1], 1))
-    q_next, lat_next = tie(q_list[2], lat_got[1])
-    q_list.append(ring(q_next, 1))
-    lat_got.append(ring(lat_next, 1))
-    q_all = gather_bits(jnp.stack(q_list), (1,), dp)
-    q_all, lat_next = tie(q_all, lat_got[2])
+    q_turned = jnp.concatenate([q_piece[:, : quarter // 2], q_piece[:, quarter // 2 :]], axis=0)
+    lat_up = jnp.concatenate([latent_own, up_piece, o_piece, q_turned], axis=1)
+    lat_got = ring_gather(lat_up)
+    o_start = 2 * lat_width + quarter
+    q_start = o_start + block
+    q_all = jnp.stack(
+        [jnp.concatenate([got[:block, q_start:], got[block:, q_start:]], axis=1) for got in lat_got]
+    )
+    q_all = gather_bits(q_all, (1,), dp)
+    o_got = jnp.concatenate([got[:, o_start:q_start] for got in lat_got], axis=0)
+    q_all, o_got = tie(q_all, o_got)
     q_all = gather_bits(q_all, (2, 0), dp)
-    lat_got.append(ring(lat_next, 1))
     latents = jnp.concatenate([got[:, : 2 * lat_width] for got in lat_got], axis=0)
     up_mine = jnp.concatenate([got[:, 2 * lat_width : 2 * lat_width + quarter] for got in lat_got], axis=1)
     up_other = swap(up_mine, "dp", 0)
@@ -365,8 +365,8 @@
 
     query_full = q_all.transpose(1, 2, 0, 4, 3, 5).reshape(model, width)
 
-    gate_weight, _ = tie(gate_weight, q_list[1])
-    up_weight, _ = tie(up_weight, q_list[3])
+    gate_weight, _ = tie(gate_weight, lat_got[1])
+    up_weight, _ = tie(up_weight, lat_got[1])
     down_weight, _ = tie(down_weight, lat_got[2])
     ff_half = gate_weight.shape[1] // 2
     ff_pad = -(-ff_half // 128) * 128
@@ -375,9 +375,10 @@
         chosen = jnp.where(core == 0, array[:, :ff_half], array[:, ff_half:])
         return jnp.pad(chosen, ((0, 0), (0, ff_pad - ff_half)))
 
+    gate_half, up_half = core_half(gate_weight), core_half(up_weight)
     down_half = lax.dynamic_slice_in_dim(down_weight, core * ff_half, ff_half, 0)
     down_turned = jnp.pad(down_half.T, ((0, 0), (0, ff_pad - ff_half)))
-    ff_own = jnp.concatenate([core_half(gate_weight), core_half(up_weight), down_turned], axis=1)
+    ff_own = jnp.concatenate([gate_half, up_half, down_turned], axis=1)
     spot = (dp >> 1) & 3
     turned_spot = xbit * 2 + ybit
     ff_a = lax.dynamic_slice_in_dim(ff_own, spot * block, block, 0)
@@ -392,21 +393,17 @@
     cut = planes // 2
     ff_early, ff_late = jnp.stack(ff_weights[:cut]), jnp.stack(ff_weights[cut:])
 
-    o_got = jnp.concatenate([got[:, 2 * lat_width + quarter :] for got in lat_got], axis=0)
     o_got = gather_bits(o_got, (1, 2, 0), dp)
     out_full = o_got.transpose(3, 1, 2, 0, 4).reshape(width, model)
 
     queries = matmul(rows_one, query_full).astype(bf16)
     keys = matmul(latents, keys_wide).astype(bf16)
     values = matmul(latents, values_wide).astype(bf16)
-    queries, out_full = tie(queries, out_full)
     info = jnp.stack([boundary] + [plane_of[k].astype(jnp.int32) * rows for k in range(planes)])
-    attended, weights = [], []
-    for half in range(2):
-        got, kept_weights = attend_forward(queries, keys, values, info, half)
-        attended.append(got)
-        weights.append(kept_weights)
-    attended = jnp.concatenate(attended, axis=1)
+    attended, first_weights = attend_forward(queries, keys, values, info, 0)
+    attended, out_full = tie(attended, out_full)
+    attended, second_weights = attend_forward(queries, keys, values, info, 1, attended)
+    weights = (first_weights, second_weights)
     mixed = inputs + matmul(attended, out_full)
     normed_two, factor_two = normalize(mixed)
     rows_two = (normed_two * feedforward_gain).astype(bf16)
@@ -494,8 +491,8 @@
 
     grad_attended, _, _ = tie(grad_attended, send_a, send_b)
 
-    def back(half, grad):
-        return attend_backward(queries, keys, values, grad, weights[half], half)
+    def back(half, grad, *started):
+        return attend_backward(queries, keys, values, grad, weights[half], half, *started)
 
     def kept_blocks(grads):
         return ff_blocks(kept, grads)
@@ -509,10 +506,7 @@
     early_next_a, early_next_b = swap(next_a, "dp", 2), swap(next_b, "dp", 1)
     own_a = rounded_sum(keep_a[:, :block], early_a[:, :block])
     own_b = rounded_sum(keep_b[:, :block], early_b[:, :block])
-    second_back = back(1, grad_attended)
-    grad_queries, grad_keys, grad_values = [
-        jnp.concatenate(pair, axis=1) for pair in zip((first_query, *first_back[1:]), second_back)
-    ]
+    grad_queries, grad_keys, grad_values = back(1, grad_attended, first_query, *first_back[1:])
     latent_part = (contract_cols(grad_keys, keys_wide) + contract_cols(grad_values, values_wide)).astype(bf16)
     late_hidden, late_act, latent_part = tie(*late_grads, latent_part)
 
@@ -540,17 +534,20 @@
 
     late_got = swap(late(one_far, far), "dp", 0)
     ff_parts = finish(rounded_sum(own_a, early_next_a), rounded_sum(own_b, early_next_b))
+    late_sum = rounded_sum(late(one_near, near), late_got)
     lat_next, ff_next = tie(rounded_sum(lat_one, lat_rows(2)), ff_parts[1])
     lat_two = ring(lat_next, -1)
     ff_next = ring(ff_next, 1)
-    late_sum = rounded_sum(late(one_near, near), late_got)
-    lat_next, late_sum = tie(rounded_sum(lat_two, lat_rows(1)), late_sum)
-    lat_three = ring(lat_next, -1)
+    lat_two, late_sum, out_part = tie(lat_two, late_sum, out_part)
+    out_grad = plane_sum(ring_columns(out_part)).T
     late_got = swap(late_sum[2:], "dp", 1)
-    grad_latent = rounded_sum(lat_three, lat_rows(0))
+    lat_three = ring(rounded_sum(lat_two, lat_rows(1)), -1)
     own_a = rounded_sum(keep_a[:, :block], late_a[:, :block])
     own_b = rounded_sum(keep_b[:, :block], late_b[:, :block])
 
+    ff_parts += finish(rounded_sum(own_a, late_next_a), rounded_sum(own_b, late_next_b))
+    grad_latent, ff_next = tie(rounded_sum(lat_three, lat_rows(0)), rounded_sum(ff_next, ff_parts[2]))
+    ff_next = ring(ff_next, 1)
     grad_one = contract_cols(grad_queries, query_full) + contract_cols(grad_latent, latent_down)
     back_one, gain_one = norm_backward(grad_one, normed_one, factor_one, attention_gain)
     tokens_grad = grad_mixed + back_one
@@ -564,21 +561,16 @@
 
     last_sum = rounded_sum(last(one_near, near), swap(last(one_far, far), "dp", 0))
     late_sum = rounded_sum(late_sum[:2], late_got)
-    ff_parts += finish(rounded_sum(own_a, late_next_a), rounded_sum(own_b, late_next_b))
-    ff_next = rounded_sum(ff_next, ff_parts[2])
-    last_sum, ff_next, late_sum, out_part = tie(last_sum, ff_next, late_sum, out_part)
-    out_grad = plane_sum(ring_columns(out_part)).T
-    ff_next = ring(ff_next, 1)
+    last_sum, late_sum = tie(last_sum, late_sum)
     last_sum = rounded_sum(last_sum[:2], swap(last_sum[2:], "dp", 1))
     late_sum = rounded_sum(late_sum[0], swap(late_sum[1], "dp", 2))
+    last_sum, ff_next = tie(last_sum, rounded_sum(ff_next, ff_parts[3]))
+    ff_total = ring(ff_next, 1).astype(f32) + ff_parts[0].astype(f32)
     last_sum = rounded_sum(last_sum[0], swap(last_sum[1], "dp", 2))
     if high > 1:
         cuts = [late_sum[:block], late_sum[block : block + lat_width // 8], late_sum[block + lat_width // 8 :]]
         late_sum = high_bits(jnp.concatenate([cut.reshape(high, -1, width) for cut in cuts], axis=1))
         last_sum = high_bits(last_sum.reshape(high, part, last_sum.shape[1]))
-    ff_next = rounded_sum(ff_next, ff_parts[3])
-    last_sum, ff_next, late_sum = tie(last_sum, ff_next, late_sum)
-    ff_total = ring(ff_next, 1).astype(f32) + ff_parts[0].astype(f32)
     lat_cols = 2 * lat_width // planes
 
     def last_columns(r):

time: 439 us -> 476 us (1.084)
  waiting for transfers between devices: 119 us -> 158 us
  starting transfers between devices: 57.1 us -> 44.6 us
  other arithmetic: 60.8 us -> 72.9 us
  local copies, waits for them, and re-layouts: 64.8 us -> 53.3 us
  Pallas kernels: 84.9 us -> 92.8 us
    ppermute x42, waiting for transfers between devices: 72.7 us -> 94 us  [swap(): return lax.ppermute(block, axis, [(i, i ^ 1 << bit) for i in range(count)])]
    ppermute x15 -> x12, waiting for transfers between devices: 46.6 us -> 64 us  [ring(): lax.ppermute(block, 'tp', [(i, (i + step) % count) for i in range(count)])]
    ppermute x42, starting transfers between devices: 38.5 us -> 30.4 us  [swap(): return lax.ppermute(block, axis, [(i, i ^ 1 << bit) for i in range(count)])]
    pallas_call x2, Pallas kernels: 28.1 us -> 35.8 us  [feed_forward(): pl.pallas_call(functools.partial(feed_kernel, len(starts) > 0, with_send)...]
    unnamed x186 -> x180, local copies, waits for them, and re-layouts: 17.4 us -> 10.5 us
    another operation x28 -> x31, other arithmetic: 11.8 us -> 16.6 us  [gather_bits(): block = jnp.stack([first, second])]
    ppermute x15 -> x12, starting transfers between devices: 18.5 us -> 14.2 us  [ring(): lax.ppermute(block, 'tp', [(i, (i + step) % count) for i in range(count)])]
    convert_element_type x19 -> x20, other arithmetic: 18.3 us -> 22.5 us  [rounded_sum(): return (left.astype(f32) + right.astype(f32)).astype(bf16)]
  transfers between devices with their start and end apart: 58 -> 55, of which waited for: 28 -> 21; matrix products, arithmetic and copies ran while one was open for 30% -> 28% of each run, Pallas kernels for 16% -> 15%
where the time goes in v1:
time: 476 us; the launch traced here: 467 us
  waiting for transfers between devices  158 us (33%)
  Pallas kernels  92.8 us (19%)
  other arithmetic  72.9 us (15%)
  local copies, waits for them, and re-layouts  53.3 us (11%)
  starting transfers between devices  44.6 us (9%)
  matrix products  28.8 us (6%)
  between operations  16.2 us (3%)
    ppermute x42, waiting for transfers between devices, swap(): return lax.ppermute(block, axis, [(i, i ^ 1 << bit) for i in range(count)])  94 us
    ppermute x12, waiting for transfers between devices, ring(): lax.ppermute(block, 'tp', [(i, (i + step) % count) for i in range(count)])  64 us
    pallas_call x2, Pallas kernels, feed_forward(): pl.pallas_call(functools.partial(feed_kernel, len(starts) > 0, with_send)...  35.8 us
    ppermute x42, starting transfers between devices, swap(): return lax.ppermute(block, axis, [(i, i ^ 1 << bit) for i in range(count)])  30.4 us
    convert_element_type x20, other arithmetic, rounded_sum(): return (left.astype(f32) + right.astype(f32)).astype(bf16)  22.5 us
    pallas_call x4, Pallas kernels, feed_grads(): pl.pallas_call(feed_grad_kernel, grid_spec=pltpu.PrefetchScalarGridSpec(n...  20.4 us
    pallas_call x2, Pallas kernels, attend_backward(): pl.pallas_call(backward_kernel, grid=(pairs,), in_specs=[part, deep, deep...  19.1 us
    pallas_call x2, Pallas kernels, attend_forward(): pl.pallas_call(forward_kernel, grid_spec=pltpu.PrefetchScalarGridSpec(num...  17.5 us
  transfers between devices with their start and end apart: 55, of which 21 were waited for; matrix products, arithmetic and copies ran while one was open for 28% of the time, Pallas kernels for 15%

profile of v1, /device:TPU:0, one launch (start us, length us, event | category | flops | bytes accessed | tf_op | source)
XLA Modules:
  0.0 466.6 jit_solution(4651240685305521762)
XLA Ops:
  12.9 3.1 collective-permute-start
  18.1 12.1 %collective-permute-done = bf16[256,1024]{1,0:T(8,128)(2,1)} collective-permute-done((bf16[256,1024]{1,0:T(8,128)(2,1)}, bf16[256,1024]{1,0:T(8,128)(2,1)}, u32[]{:S(2)}, u32[]{:S(2)}) %collective-permute-start) | collective-permute-done | bytes 524320 | tf_op jit(solution)/shard_map/ppermute | solution.py:48
  45.1 5.5 %collective-permute-done.1 = bf16[256,1024]{1,0:T(8,128)(2,1)} collective-permute-done((bf16[256,1024]{1,0:T(8,128)(2,1)}, bf16[256,1024]{1,0:T(8,128)(2,1)}, u32[]{:S(2)}, u32[]{:S(2)}) %collective-permute-start.1) | collective-permute-done | bytes 524320 | tf_op jit(solution)/shard_map/ppermute | solution.py:48
  59.0 11.2 %collective-permute-done.2 = bf16[256,1024]{1,0:T(8,128)(2,1)S(1)} collective-permute-done((bf16[256,1024]{1,0:T(8,128)(2,1)}, bf16[256,1024]{1,0:T(8,128)(2,1)S(1)}, u32[]{:S(2)}, u32[]{:S(2)}) %collective-permute-start.2) | collective-permute-done | bytes 524320 | tf_op jit(solution)/shard_map/ppermute | solution.py:48
  71.5 6.0 %collective-permute-done.3 = bf16[4,128,256]{2,1,0:T(8,128)(2,1)S(1)} collective-permute-done((bf16[4,128,256]{2,1,0:T(8,128)(2,1)S(1)}, bf16[4,128,256]{2,1,0:T(8,128)(2,1)S(1)}, u32[]{:S(2)}, u32[]{:S(2)}) %collective-permute-start.3) | collective-permute-done | bytes 262176 | tf_op jit(solution)/shard_map/ppermute | solution.py:43
  80.8 3.2 collective-permute-done.7
  91.8 4.9 %collective-permute-done.12 = bf16[256,1152]{1,0:T(8,128)(2,1)S(1)} collective-permute-done((bf16[256,1152]{1,0:T(8,128)(2,1)S(1)}, bf16[256,1152]{1,0:T(8,128)(2,1)S(1)}, u32[]{:S(2)}, u32[]{:S(2)}) %collective-permute-start.12) | collective-permute-done | bytes 589856 | tf_op jit(solution)/shard_map/ppermute | solution.py:48
  99.2 6.2 %collective-permute-done.13 = bf16[128,1152]{1,0:T(8,128)(2,1)S(1)} collective-permute-done((bf16[128,1152]{1,0:T(8,128)(2,1)S(1)}, bf16[128,1152]{1,0:T(8,128)(2,1)S(1)}, u32[]{:S(2)}, u32[]{:S(2)}) %collective-permute-start.13) | collective-permute-done | bytes 294944 | tf_op jit(solution)/shard_map/ppermute | solution.py:43
  105.4 5.8 %collective-permute-done.15 = bf16[128,1152]{1,0:T(8,128)(2,1)S(1)} collective-permute-done((bf16[128,1152]{1,0:T(8,128)(2,1)S(1)}, bf16[128,1152]{1,0:T(8,128)(2,1)S(1)}, u32[]{:S(2)}, u32[]{:S(2)}) %collective-permute-start.15) | collective-permute-done | bytes 294944 | tf_op jit(solution)/shard_map/ppermute | solution.py:43
  118.2 15.8 %collective-permute-done.18 = bf16[128,1152]{1,0:T(8,128)(2,1)S(1)} collective-permute-done((bf16[128,1152]{1,0:T(8,128)(2,1)S(1)}, bf16[128,1152]{1,0:T(8,128)(2,1)S(1)}, u32[]{:S(2)}, u32[]{:S(2)}) %collective-permute-start.18) | collective-permute-done | bytes 294944 | tf_op jit(solution)/shard_map/ppermute | solution.py:43
  141.0 10.8 %collective-permute-done.22 = bf16[256,1152]{1,0:T(8,128)(2,1)S(1)} collective-permute-done((bf16[256,1152]{1,0:T(8,128)(2,1)S(1)}, bf16[256,1152]{1,0:T(8,128)(2,1)S(1)}, u32[]{:S(2)}, u32[]{:S(2)}) %collective-permute-start.22) | collective-permute-done | bytes 589856 | tf_op jit(solution)/shard_map/ppermute | solution.py:48
  159.3 8.7 %attend_forward.2 = (bf16[256,1024]{1,0:T(8,128)(2,1)}, bf16[8,256,1024]{2,1,0:T(8,128)(2,1)}) custom-call(s32[5]{0:T(128)} %stack.287.info, bf16[256,1024]{1,0:T(8,128)(2,1)} %convolution_convert_fusion.8.q_ref, bf16[1024,1024]{1,0:T(8,128)(2,1)} %convolution_convert_fusion.2.k_ref, bf16[1024,1024]{1,0:T(8,128)(2,1)} %convolution_convert_fusion.1.v_ref), custom_call_target="tpu_custom_call" | custom-call | tf_op jit(solution)/shard_map/attend_forward/pallas_call | solution.py:128
  184.8 8.8 %attend_forward.3 = (bf16[256,1024]{1,0:T(8,128)(2,1)}, bf16[8,256,1024]{2,1,0:T(8,128)(2,1)}) custom-call(s32[5]{0:T(128)} %stack.287.info, bf16[256,1024]{1,0:T(8,128)(2,1)} %convolution_convert_fusion.8.q_ref, bf16[1024,1024]{1,0:T(8,128)(2,1)} %convolution_convert_fusion.2.k_ref, ...), custom_call_target="tpu_custom_call", output_to_operand_aliasing={{0}: (4, {})} | custom-call | tf_op jit(solution)/shard_map/attend_forward/pallas_call | solution.py:128
  200.0 13.7 %feed_forward.2 = (bf16[2,512,768]{2,1,0:T(8,128)(2,1)}, bf16[2,512,384]{2,1,0:T(8,128)(2,1)}, f32[512,1024]{1,0:T(8,128)}, f32[512,1024]{1,0:T(8,128)}, bf16[10...) custom-call(bf16[512,1024]{1,0:T(8,128)(2,1)} %pad_maximum_fusion.13.refs_0_, bf16[512,1024]{1,0:T(8,128)(2,1)} %copy-done.9, ...), custom_call_target="tpu_custom_call" | custom-call | tf_op jit(solution)/shard_map/feed_forward/pallas_call | solution.py:222
  213.7 5.2 %feed_grads.4 = (bf16[2,256,1152]{2,1,0:T(8,128)(2,1)}, bf16[2,256,1152]{2,1,0:T(8,128)(2,1)}) custom-call(s32[4]{0:T(128)} %get-tuple-element.304.spots, bf16[1024,512]{1,0:T(8,128)(2,1)} %get-tuple-element.87.refs_0_.refs_1_.refs_2_.refs_3_, bf16[1024,512]{1,0:T(8,128)(2,1)} %get-tuple-element.87.refs_0_.refs_1_.refs_2_.refs_3_, ...), custom_call_target="tpu_custom_call" | custom-call | tf_op jit(solution)/shard_map/feed_grads/pallas_call | solution.py:264
  226.1 22.1 %feed_forward.3 = (bf16[2,512,768]{2,1,0:T(8,128)(2,1)}, bf16[2,512,384]{2,1,0:T(8,128)(2,1)}, f32[512,1024]{1,0:T(8,128)}, f32[512,1024]{1,0:T(8,128)}, bf16[25...) custom-call(bf16[512,1024]{1,0:T(8,128)(2,1)} %pad_maximum_fusion.13.refs_0_, bf16[512,1024]{1,0:T(8,128)(2,1)} %copy-done.9, ...), custom_call_target="tpu_custom_call" | custom-call | tf_op jit(solution)/shard_map/feed_forward/pallas_call | solution.py:222
  251.9 5.0 %feed_grads.5 = (bf16[2,256,1152]{2,1,0:T(8,128)(2,1)}, bf16[2,256,1152]{2,1,0:T(8,128)(2,1)}) custom-call(s32[4]{0:T(128)} %get-tuple-element.304.spots, bf16[1024,512]{1,0:T(8,128)(2,1)} %get-tuple-element.87.refs_0_.refs_1_.refs_2_.refs_3_, bf16[1024,512]{1,0:T(8,128)(2,1)} %get-tuple-element.87.refs_0_.refs_1_.refs_2_.refs_3_, ...), custom_call_target="tpu_custom_call" | custom-call | tf_op jit(solution)/shard_map/feed_grads/pallas_call | solution.py:264
  261.9 3.2 multiply_add_fusion
  266.6 9.5 %attend_backward.2 = (bf16[256,1024]{1,0:T(8,128)(2,1)}, bf16[1024,1024]{1,0:T(8,128)(2,1)}, bf16[1024,1024]{1,0:T(8,128)(2,1)}) custom-call(bf16[256,1024]{1,0:T(8,128)(2,1)} %convolution_convert_fusion.8.q_ref, bf16[1024,1024]{1,0:T(8,128)(2,1)} %convolution_convert_fusion.2.k_ref, bf16[1024,1024]{1,0:T(8,128)(2,1)} %convolution_convert_fusion.1.v_ref, ...), custom_call_target="tpu_custom_call" | custom-call | tf_op jit(solution)/shard_map/attend_backward/pallas_call | solution.py:153
  278.3 5.1 %feed_grads.6 = (bf16[2,256,1152]{2,1,0:T(8,128)(2,1)}, bf16[2,256,1152]{2,1,0:T(8,128)(2,1)}) custom-call(s32[4]{0:T(128)} %get-tuple-element.305.spots, bf16[1024,512]{1,0:T(8,128)(2,1)} %get-tuple-element.87.refs_0_.refs_1_.refs_2_.refs_3_, bf16[1024,512]{1,0:T(8,128)(2,1)} %get-tuple-element.87.refs_0_.refs_1_.refs_2_.refs_3_, ...), custom_call_target="tpu_custom_call" | custom-call | tf_op jit(solution)/shard_map/feed_grads/pallas_call | solution.py:264
  287.8 9.6 %attend_backward.3 = (bf16[256,1024]{1,0:T(8,128)(2,1)}, bf16[1024,1024]{1,0:T(8,128)(2,1)}, bf16[1024,1024]{1,0:T(8,128)(2,1)}) custom-call(bf16[256,1024]{1,0:T(8,128)(2,1)} %convolution_convert_fusion.8.q_ref, bf16[1024,1024]{1,0:T(8,128)(2,1)} %convolution_convert_fusion.2.k_ref, ...), custom_call_target="tpu_custom_call", output_to_operand_aliasing={{0}: (5, {}), {1}: (6, {}), {2}: (7, {})} | custom-call | tf_op jit(solution)/shard_map/attend_backward/pallas_call | solution.py:153
  297.4 3.3 fusion.22
  303.0 5.1 %feed_grads.7 = (bf16[2,256,1152]{2,1,0:T(8,128)(2,1)}, bf16[2,256,1152]{2,1,0:T(8,128)(2,1)}) custom-call(s32[4]{0:T(128)} %get-tuple-element.305.spots, bf16[1024,512]{1,0:T(8,128)(2,1)} %get-tuple-element.87.refs_0_.refs_1_.refs_2_.refs_3_, bf16[1024,512]{1,0:T(8,128)(2,1)} %get-tuple-element.87.refs_0_.refs_1_.refs_2_.refs_3_, ...), custom_call_target="tpu_custom_call" | custom-call | tf_op jit(solution)/shard_map/feed_grads/pallas_call | solution.py:264
  308.2 3.2 fusion.59
  328.0 17.0 %collective-permute-done.32 = bf16[2,128,1152]{2,1,0:T(8,128)(2,1)S(1)} collective-permute-done((bf16[2,128,1152]{2,1,0:T(8,128)(2,1)S(1)}, bf16[2,128,1152]{2,1,0:T(8,128)(2,1)S(1)}, u32[]{:S(2)}, u32[]{:S(2)}) %collective-permute-start.32) | collective-permute-done | bytes 589856 | tf_op jit(solution)/shard_map/ppermute | solution.py:43
  350.8 3.0 collective-permute-start.34
  359.5 10.9 %collective-permute-done.34 = bf16[256,512]{1,0:T(8,128)(2,1)S(1)} collective-permute-done((bf16[256,512]{1,0:T(8,128)(2,1)S(1)}, bf16[256,512]{1,0:T(8,128)(2,1)S(1)}, u32[]{:S(2)}, u32[]{:S(2)}) %collective-permute-start.34) | collective-permute-done | bytes 262176 | tf_op jit(solution)/shard_map/ppermute | solution.py:48
  379.0 7.9 %collective-permute-done.50 = bf16[128,512]{1,0:T(8,128)(2,1)S(1)} collective-permute-done((bf16[128,512]{1,0:T(8,128)(2,1)S(1)}, bf16[128,512]{1,0:T(8,128)(2,1)S(1)}, u32[]{:S(2)}, u32[]{:S(2)}) %collective-permute-start.50) | collective-permute-done | bytes 131104 | tf_op jit(solution)/shard_map/ppermute | solution.py:43
  403.8 5.1 %collective-permute-done.45 = bf16[2,128,1152]{2,1,0:T(8,128)(2,1)} collective-permute-done((bf16[2,128,1152]{2,1,0:T(8,128)(2,1)}, bf16[2,128,1152]{2,1,0:T(8,128)(2,1)}, u32[]{:S(2)}, u32[]{:S(2)}) %collective-permute-start.45) | collective-permute-done | bytes 589856 | tf_op jit(solution)/shard_map/ppermute | solution.py:48
  414.8 7.3 %collective-permute-done.47 = bf16[192,1024]{1,0:T(8,128)(2,1)S(1)} collective-permute-done((bf16[192,1024]{1,0:T(8,128)(2,1)S(1)}, bf16[192,1024]{1,0:T(8,128)(2,1)S(1)}, u32[]{:S(2)}, u32[]{:S(2)}) %collective-permute-start.47) | collective-permute-done | bytes 393248 | tf_op jit(solution)/shard_map/ppermute | solution.py:43
  427.1 18.1 %collective-permute-done.48 = bf16[320,512]{1,0:T(8,128)(2,1)} collective-permute-done((bf16[320,512]{1,0:T(8,128)(2,1)}, bf16[320,512]{1,0:T(8,128)(2,1)}, u32[]{:S(2)}, u32[]{:S(2)}) %collective-permute-start.48) | collective-permute-done | bytes 327712 | tf_op jit(solution)/shard_map/ppermute | solution.py:43
  448.9 3.5 collective-permute-done.49
  (444 shorter events, 190.8 us)
Async XLA Ops:
  7.2 363.2 %reduce-scatter.2.cloned.1.call-start = ((), (), s32[]{:S(2)}) async-start(), calls=%async_computation.1 | async-start | bytes 2359296 | tf_op jit(solution)/shard_map/reduce_scatter | solution.py:490
  12.9 17.3 %collective-permute-start = (bf16[256,1024]{1,0:T(8,128)(2,1)}, bf16[256,1024]{1,0:T(8,128)(2,1)}, u32[]{:S(2)}, u32[]{:S(2)}) collective-permute-start(bf16[256,1024]{1,0:T(8,128)(2,1)} %maximum_maximum_fusion.1), channel_id=1, source_target_pairs={{0,1},{1,2},{2,3},{3,0},{4,5},{5,6},{6,7},{7,4},{8,9},{9,10},{10,1... | collective-permute-start | bytes 1572872 | tf_op jit(solution)/shard_map/ppermute | solution.py:48
  16.0 23.6 %collective-permute-start.11 = (bf16[256,1024]{1,0:T(8,128)(2,1)S(1)}, bf16[256,1024]{1,0:T(8,128)(2,1)}, u32[]{:S(2)}, u32[]{:S(2)}) collective-permute-start(bf16[256,1024]{1,0:T(8,128)(2,1)S(1)} %copy-done.37), channel_id=1, source_target_pairs={{0,4},{4,0},{8,12},{12,8},{16,20},{20,16},{24,28},{28,24},{1,5},{5... | collective-permute-start | bytes 1572872 | tf_op jit(solution)/shard_map/ppermute | solution.py:43
  79.1 17.6 %collective-permute-start.12 = (bf16[256,1152]{1,0:T(8,128)(2,1)S(1)}, bf16[256,1152]{1,0:T(8,128)(2,1)S(1)}, u32[]{:S(2)}, u32[]{:S(2)}) collective-permute-start(bf16[256,1152]{1,0:T(8,128)(2,1)S(1)} %pad_maximum_fusion.18), channel_id=1, source_target_pairs={{0,1},{1,2},{2,3},{3,0},{4,5},{5,6},{6,7},{7,4},{8,9},{9,10},{10,1... | collective-permute-start | bytes 1769480 | tf_op jit(solution)/shard_map/ppermute | solution.py:48
  79.2 19.6 %collective-permute-start.4 = (bf16[2,4,128,256]{3,2,1,0:T(8,128)(2,1)S(1)}, bf16[2,4,128,256]{3,2,1,0:T(8,128)(2,1)S(1)}, u32[]{:S(2)}, u32[]{:S(2)}) collective-permute-start(bf16[2,4,128,256]{3,2,1,0:T(8,128)(2,1)S(1)} %pad_maximum_fusion.26), channel_id=1, source_target_pairs={{0,16},{4,20},{8,24},{12,28},{16,0},{20,4},{24,8},{28,12},{1,17},{... | collective-permute-start | bytes 1572872 | tf_op jit(solution)/shard_map/ppermute | solution.py:43
  84.2 32.4 %collective-permute-start.8 = (bf16[2,1024,128]{2,1,0:T(8,128)(2,1)S(1)}, bf16[2,1024,128]{2,1,0:T(8,128)(2,1)S(1)}, u32[]{:S(2)}, u32[]{:S(2)}) collective-permute-start(bf16[2,1024,128]{2,1,0:T(8,128)(2,1)S(1)} %pad_maximum_fusion.28), channel_id=1, source_target_pairs={{0,16},{4,20},{8,24},{12,28},{16,0},{20,4},{24,8},{28,12},{1,17},{... | collective-permute-start | bytes 1572872 | tf_op jit(solution)/shard_map/ppermute | solution.py:43
  99.1 54.2 %collective-permute-start.5 = (bf16[2,2,4,128,256]{4,3,2,1,0:T(8,128)(2,1)S(1)}, bf16[2,2,4,128,256]{4,3,2,1,0:T(8,128)(2,1)S(1)}, u32[]{:S(2)}, u32[]{:S(2)}) collective-permute-start(bf16[2,2,4,128,256]{4,3,2,1,0:T(8,128)(2,1)S(1)} %pad_maximum_fusion.8), channel_id=1, source_target_pairs={{0,4},{4,0},{8,12},{12,8},{16,20},{20,16},{24,28},{28,24},{1,5},{5... | collective-permute-start | bytes 3145736 | tf_op jit(solution)/shard_map/ppermute | solution.py:43
  111.4 24.1 %collective-permute-start.14 = (bf16[2,128,1152]{2,1,0:T(8,128)(2,1)S(1)}, bf16[2,128,1152]{2,1,0:T(8,128)(2,1)S(1)}, u32[]{:S(2)}, u32[]{:S(2)}) collective-permute-start(bf16[2,128,1152]{2,1,0:T(8,128)(2,1)S(1)} %pad_maximum_fusion.19), channel_id=1, source_target_pairs={{0,16},{4,20},{8,24},{12,28},{16,0},{20,4},{24,8},{28,12},{1,17},{... | collective-permute-start | bytes 1769480 | tf_op jit(solution)/shard_map/ppermute | solution.py:43
  113.0 24.1 %collective-permute-start.16 = (bf16[2,128,1152]{2,1,0:T(8,128)(2,1)S(1)}, bf16[2,128,1152]{2,1,0:T(8,128)(2,1)S(1)}, u32[]{:S(2)}, u32[]{:S(2)}) collective-permute-start(bf16[2,128,1152]{2,1,0:T(8,128)(2,1)S(1)} %pad_maximum_fusion.20), channel_id=1, source_target_pairs={{0,8},{4,12},{8,0},{12,4},{16,24},{20,28},{24,16},{28,20},{1,9},{5... | collective-permute-start | bytes 1769480 | tf_op jit(solution)/shard_map/ppermute | solution.py:43
  115.0 19.0 %collective-permute-start.18 = (bf16[128,1152]{1,0:T(8,128)(2,1)S(1)}, bf16[128,1152]{1,0:T(8,128)(2,1)S(1)}, u32[]{:S(2)}, u32[]{:S(2)}) collective-permute-start(bf16[128,1152]{1,0:T(8,128)(2,1)S(1)} %get-tuple-element.230), channel_id=1, source_target_pairs={{0,8},{4,12},{8,0},{12,4},{16,24},{20,28},{24,16},{28,20},{1,9},{5... | collective-permute-start | bytes 884744 | tf_op jit(solution)/shard_map/ppermute | solution.py:43
  116.6 17.4 %collective-permute-start.20 = (bf16[128,1152]{1,0:T(8,128)(2,1)S(1)}, bf16[128,1152]{1,0:T(8,128)(2,1)S(1)}, u32[]{:S(2)}, u32[]{:S(2)}) collective-permute-start(bf16[128,1152]{1,0:T(8,128)(2,1)S(1)} %get-tuple-element.231), channel_id=1, source_target_pairs={{0,16},{4,20},{8,24},{12,28},{16,0},{20,4},{24,8},{28,12},{1,17},{... | collective-permute-start | bytes 884744 | tf_op jit(solution)/shard_map/ppermute | solution.py:43
  134.0 44.8 %collective-permute-start.9 = (bf16[2,2,1024,128]{3,2,1,0:T(8,128)(2,1)}, bf16[2,2,1024,128]{3,2,1,0:T(8,128)(2,1)}, u32[]{:S(2)}, u32[]{:S(2)}) collective-permute-start(bf16[2,2,1024,128]{3,2,1,0:T(8,128)(2,1)} %pad_maximum_fusion.12), channel_id=1, source_target_pairs={{0,4},{4,0},{8,12},{12,8},{16,20},{20,16},{24,28},{28,24},{1,5},{5... | collective-permute-start | bytes 3145736 | tf_op jit(solution)/shard_map/ppermute | solution.py:43
  134.0 17.8 %collective-permute-start.22 = (bf16[256,1152]{1,0:T(8,128)(2,1)S(1)}, bf16[256,1152]{1,0:T(8,128)(2,1)S(1)}, u32[]{:S(2)}, u32[]{:S(2)}) collective-permute-start(bf16[256,1152]{1,0:T(8,128)(2,1)S(1)} %collective-permute-done.17), channel_id=1, source_target_pairs={{0,1},{1,2},{2,3},{3,0},{4,5},{5,6},{6,7},{7,4},{8,9},{9,10},{10,1... | collective-permute-start | bytes 1769480 | tf_op jit(solution)/shard_map/ppermute | solution.py:48
  135.4 38.7 %collective-permute-start.19 = (bf16[2,128,1152]{2,1,0:T(8,128)(2,1)}, bf16[2,128,1152]{2,1,0:T(8,128)(2,1)}, u32[]{:S(2)}, u32[]{:S(2)}) collective-permute-start(bf16[2,128,1152]{2,1,0:T(8,128)(2,1)} %pad_maximum_fusion.21), channel_id=1, source_target_pairs={{0,16},{4,20},{8,24},{12,28},{16,0},{20,4},{24,8},{28,12},{1,17},{... | collective-permute-start | bytes 1769480 | tf_op jit(solution)/shard_map/ppermute | solution.py:43
  137.1 39.5 %collective-permute-start.21 = (bf16[2,128,1152]{2,1,0:T(8,128)(2,1)}, bf16[2,128,1152]{2,1,0:T(8,128)(2,1)}, u32[]{:S(2)}, u32[]{:S(2)}) collective-permute-start(bf16[2,128,1152]{2,1,0:T(8,128)(2,1)} %pad_maximum_fusion.22), channel_id=1, source_target_pairs={{0,8},{4,12},{8,0},{12,4},{16,24},{20,28},{24,16},{28,20},{1,9},{5... | collective-permute-start | bytes 1769480 | tf_op jit(solution)/shard_map/ppermute | solution.py:43
  170.5 48.4 %collective-permute-start.24 = (bf16[2,128,1152]{2,1,0:T(8,128)(2,1)}, bf16[2,128,1152]{2,1,0:T(8,128)(2,1)}, u32[]{:S(2)}, u32[]{:S(2)}) collective-permute-start(bf16[2,128,1152]{2,1,0:T(8,128)(2,1)} %pad_maximum_fusion.23), channel_id=1, source_target_pairs={{0,16},{4,20},{8,24},{12,28},{16,0},{20,4},{24,8},{28,12},{1,17},{... | collective-permute-start | bytes 1769480 | tf_op jit(solution)/shard_map/ppermute | solution.py:43
  172.7 47.7 %collective-permute-start.26 = (bf16[2,128,1152]{2,1,0:T(8,128)(2,1)}, bf16[2,128,1152]{2,1,0:T(8,128)(2,1)}, u32[]{:S(2)}, u32[]{:S(2)}) collective-permute-start(bf16[2,128,1152]{2,1,0:T(8,128)(2,1)} %pad_maximum_fusion.24), channel_id=1, source_target_pairs={{0,8},{4,12},{8,0},{12,4},{16,24},{20,28},{24,16},{28,20},{1,9},{5... | collective-permute-start | bytes 1769480 | tf_op jit(solution)/shard_map/ppermute | solution.py:43
  250.6 32.7 %collective-permute-start.30 = (bf16[2,256,1152]{2,1,0:T(8,128)(2,1)}, bf16[2,256,1152]{2,1,0:T(8,128)(2,1)}, u32[]{:S(2)}, u32[]{:S(2)}) collective-permute-start(bf16[2,256,1152]{2,1,0:T(8,128)(2,1)} %get-tuple-element.112), channel_id=1, source_target_pairs={{0,16},{4,20},{8,24},{12,28},{16,0},{20,4},{24,8},{28,12},{1,17},{... | collective-permute-start | bytes 3538952 | tf_op jit(solution)/shard_map/ppermute | solution.py:43
  251.2 34.5 %collective-permute-start.29 = (bf16[2,256,1152]{2,1,0:T(8,128)(2,1)}, bf16[2,256,1152]{2,1,0:T(8,128)(2,1)}, u32[]{:S(2)}, u32[]{:S(2)}) collective-permute-start(bf16[2,256,1152]{2,1,0:T(8,128)(2,1)} %get-tuple-element.110), channel_id=1, source_target_pairs={{0,8},{4,12},{8,0},{12,4},{16,24},{20,28},{24,16},{28,20},{1,9},{5... | collective-permute-start | bytes 3538952 | tf_op jit(solution)/shard_map/ppermute | solution.py:43
  256.9 57.7 %collective-permute-start.36 = (bf16[2,256,1152]{2,1,0:T(8,128)(2,1)}, bf16[2,256,1152]{2,1,0:T(8,128)(2,1)}, u32[]{:S(2)}, u32[]{:S(2)}) collective-permute-start(bf16[2,256,1152]{2,1,0:T(8,128)(2,1)} %get-tuple-element.103), channel_id=1, source_target_pairs={{0,16},{4,20},{8,24},{12,28},{16,0},{20,4},{24,8},{28,12},{1,17},{... | collective-permute-start | bytes 3538952 | tf_op jit(solution)/shard_map/ppermute | solution.py:43
  258.3 57.7 %collective-permute-start.35 = (bf16[2,256,1152]{2,1,0:T(8,128)(2,1)}, bf16[2,256,1152]{2,1,0:T(8,128)(2,1)}, u32[]{:S(2)}, u32[]{:S(2)}) collective-permute-start(bf16[2,256,1152]{2,1,0:T(8,128)(2,1)} %get-tuple-element.102), channel_id=1, source_target_pairs={{0,8},{4,12},{8,0},{12,4},{16,24},{20,28},{24,16},{28,20},{1,9},{5... | collective-permute-start | bytes 3538952 | tf_op jit(solution)/shard_map/ppermute | solution.py:43
  317.3 36.5 %collective-permute-start.40 = (bf16[2,128,1152]{2,1,0:T(8,128)(2,1)S(1)}, bf16[2,128,1152]{2,1,0:T(8,128)(2,1)S(1)}, u32[]{:S(2)}, u32[]{:S(2)}) collective-permute-start(bf16[2,128,1152]{2,1,0:T(8,128)(2,1)S(1)} %add_convert_fusion.11), channel_id=1, source_target_pairs={{0,16},{4,20},{8,24},{12,28},{16,0},{20,4},{24,8},{28,12},{1,17},{... | collective-permute-start | bytes 1769480 | tf_op jit(solution)/shard_map/ppermute | solution.py:43
  318.1 37.7 %collective-permute-start.41 = (bf16[2,128,1152]{2,1,0:T(8,128)(2,1)S(1)}, bf16[2,128,1152]{2,1,0:T(8,128)(2,1)S(1)}, u32[]{:S(2)}, u32[]{:S(2)}) collective-permute-start(bf16[2,128,1152]{2,1,0:T(8,128)(2,1)S(1)} %add_convert_fusion.10), channel_id=1, source_target_pairs={{0,8},{4,12},{8,0},{12,4},{16,24},{20,28},{24,16},{28,20},{1,9},{5... | collective-permute-start | bytes 1769480 | tf_op jit(solution)/shard_map/ppermute | solution.py:43
  319.0 25.9 %collective-permute-start.32 = (bf16[2,128,1152]{2,1,0:T(8,128)(2,1)S(1)}, bf16[2,128,1152]{2,1,0:T(8,128)(2,1)S(1)}, u32[]{:S(2)}, u32[]{:S(2)}) collective-permute-start(bf16[2,128,1152]{2,1,0:T(8,128)(2,1)S(1)} %copy-done.52), channel_id=1, source_target_pairs={{0,16},{4,20},{8,24},{12,28},{16,0},{20,4},{24,8},{28,12},{1,17},{... | collective-permute-start | bytes 1769480 | tf_op jit(solution)/shard_map/ppermute | solution.py:43
  320.1 26.9 %collective-permute-start.33 = (bf16[2,128,1152]{2,1,0:T(8,128)(2,1)S(1)}, bf16[2,128,1152]{2,1,0:T(8,128)(2,1)S(1)}, u32[]{:S(2)}, u32[]{:S(2)}) collective-permute-start(bf16[2,128,1152]{2,1,0:T(8,128)(2,1)S(1)} %copy-done.51), channel_id=1, source_target_pairs={{0,8},{4,12},{8,0},{12,4},{16,24},{20,28},{24,16},{28,20},{1,9},{5... | collective-permute-start | bytes 1769480 | tf_op jit(solution)/shard_map/ppermute | solution.py:43
  327.9 30.0 %collective-permute-start.37 = (bf16[4,192,1024]{2,1,0:T(8,128)(2,1)S(1)}, bf16[4,192,1024]{2,1,0:T(8,128)(2,1)S(1)}, u32[]{:S(2)}, u32[]{:S(2)}) collective-permute-start(bf16[4,192,1024]{2,1,0:T(8,128)(2,1)S(1)} %maximum_maximum_fusion), channel_id=1, source_target_pairs={{0,4},{4,0},{8,12},{12,8},{16,20},{20,16},{24,28},{28,24},{1,5},{5... | collective-permute-start | bytes 4718600 | tf_op jit(solution)/shard_map/ppermute | solution.py:43
  349.9 26.2 %collective-permute-start.39 = (bf16[2,128,1152]{2,1,0:T(8,128)(2,1)}, bf16[2,128,1152]{2,1,0:T(8,128)(2,1)S(1)}, u32[]{:S(2)}, u32[]{:S(2)}) collective-permute-start(bf16[2,128,1152]{2,1,0:T(8,128)(2,1)} %pad_maximum_fusion.25), channel_id=1, source_target_pairs={{0,1},{1,2},{2,3},{3,0},{4,5},{5,6},{6,7},{7,4},{8,9},{9,10},{10,1... | collective-permute-start | bytes 1769480 | tf_op jit(solution)/shard_map/ppermute | solution.py:48
  350.8 19.6 %collective-permute-start.34 = (bf16[256,512]{1,0:T(8,128)(2,1)S(1)}, bf16[256,512]{1,0:T(8,128)(2,1)S(1)}, u32[]{:S(2)}, u32[]{:S(2)}) collective-permute-start(bf16[256,512]{1,0:T(8,128)(2,1)S(1)} %add_convert_fusion.22), channel_id=1, source_target_pairs={{0,3},{1,0},{2,1},{3,2},{4,7},{5,4},{6,5},{7,6},{8,11},{9,8},{10,9... | collective-permute-start | bytes 786440 | tf_op jit(solution)/shard_map/ppermute | solution.py:48
  378.1 23.6 %collective-permute-start.43 = (bf16[2,192,1024]{2,1,0:T(8,128)(2,1)}, bf16[2,192,1024]{2,1,0:T(8,128)(2,1)}, u32[]{:S(2)}, u32[]{:S(2)}) collective-permute-start(bf16[2,192,1024]{2,1,0:T(8,128)(2,1)} %slice.340), channel_id=1, source_target_pairs={{0,8},{4,12},{8,0},{12,4},{16,24},{20,28},{24,16},{28,20},{1,9},{5... | collective-permute-start | bytes 2359304 | tf_op jit(solution)/shard_map/ppermute | solution.py:43
  388.5 36.9 %collective-permute-start.51 = (bf16[128,256]{1,0:T(8,128)(2,1)}, bf16[128,256]{1,0:T(8,128)(2,1)}, u32[]{:S(2)}, u32[]{:S(2)}) collective-permute-start(bf16[128,256]{1,0:T(8,128)(2,1)} %add_convert_fusion.24), channel_id=1, source_target_pairs={{0,1},{1,0},{2,3},{3,2},{4,5},{5,4},{6,7},{7,6},{8,9},{9,8},{10,11... | collective-permute-start | bytes 196616 | tf_op jit(solution)/shard_map/ppermute | solution.py:43
  414.0 32.2 %collective-permute-start.52 = (bf16[2,128,1152]{2,1,0:T(8,128)(2,1)}, bf16[2,128,1152]{2,1,0:T(8,128)(2,1)}, u32[]{:S(2)}, u32[]{:S(2)}) collective-permute-start(bf16[2,128,1152]{2,1,0:T(8,128)(2,1)} %add_convert_fusion.4), channel_id=1, source_target_pairs={{0,1},{1,2},{2,3},{3,0},{4,5},{5,6},{6,7},{7,4},{8,9},{9,10},{10,1... | collective-permute-start | bytes 1769480 | tf_op jit(solution)/shard_map/ppermute | solution.py:48
  424.7 20.4 %collective-permute-start.48 = (bf16[320,512]{1,0:T(8,128)(2,1)}, bf16[320,512]{1,0:T(8,128)(2,1)}, u32[]{:S(2)}, u32[]{:S(2)}) collective-permute-start(bf16[320,512]{1,0:T(8,128)(2,1)} %maximum_maximum_fusion.2), channel_id=1, source_target_pairs={{0,2},{1,3},{2,0},{3,1},{4,6},{5,7},{6,4},{7,5},{8,10},{9,11},{10,... | collective-permute-start | bytes 983048 | tf_op jit(solution)/shard_map/ppermute | solution.py:43
  (110 other events, 894.7 us)
Sparse Core Ops, SparseCore 0:
  278.4 42.7 reduce-scatter.1
